TPU v7x, 256 devices: a whole 4x4x8 slice. The times are simulated.
256 devices in a mesh: blk: 64 (over y, z, core), band: 4 (over x).
Axes of the slice: x: 4, y: 4, z: 8, core: 2. Of those that a mesh axis runs over, the one named last changes fastest.
Arguments:
- grid_nodes: bfloat16 [131072, 512], P(('blk', 'band')), may hold values from -6 to 6
- enc_edges: bfloat16 [262144, 512], P(('blk', 'band')), may hold values from -6 to 6
- enc_sender: int32 [262144], P(('blk', 'band')), may hold values from 0 to 511, as said below
- enc_slot: int32 [262144], P(('blk', 'band')), may hold values from 0 to 511
- enc_slot_node: int32 [256, 512], P(('blk', 'band')), may hold values from 0 to 639
- mesh_nodes: bfloat16 [40960, 512], P('blk'), may hold values from -6 to 6
- mesh_edges: bfloat16 [262144, 512], P(('blk', 'band')), may hold values from -6 to 6
- mesh_sender: int32 [262144], P(('blk', 'band')), may hold values from 0 to 511
- mesh_receiver: int32 [262144], P(('blk', 'band')), may hold values from 0 to 639
- mesh_send_node: int32 [256, 512], P(('blk', 'band')), may hold values from 0 to 639
- grid_weights: bfloat16 [2, 512, 512], replicated, may hold values from -0.25 to 0.25
- enc_edge_weights: bfloat16 [4, 512, 512], replicated, may hold values from -0.25 to 0.25
- enc_node_weights: bfloat16 [3, 512, 512], replicated, may hold values from -0.25 to 0.25
- proc_edge_weights: bfloat16 [4, 512, 512], replicated, may hold values from -0.25 to 0.25
- proc_node_weights: bfloat16 [3, 512, 512], replicated, may hold values from -0.25 to 0.25
- biases: float32 [5, 2, 512], replicated, may hold values from -3 to 3
- gains: float32 [5, 512], replicated, may hold values from 0.5 to 1.5
Outputs:
- grid_out: bfloat16 [131072, 512], P(('blk', 'band'))
- mesh_out: bfloat16 [40960, 512], P(('blk', 'band'))
Inputs may be any that keep to these rules, and one draw needn't show every extreme that they name: `enc_sender`: within each device's 1024 edges the values never fall, and every one of the device's 512 grid rows is a sender.
All inputs are finite; a program needn't handle non-finite values.
Results may differ from a plain program's by a relative error of at most 0.014.
Values may be sent and summed in bfloat16 or wider, within the bound.
A program may use at most 64 MiB of HBM per device.

v0:
```python
import jax
import jax.numpy as jnp
from jax import lax
from jax.sharding import PartitionSpec as P

NEIGH = 8
CAP = 64


def shifted(block, axis, distance):
    devices = range(lax.axis_size(axis))
    route = [((i - distance) % len(devices), i) for i in devices]
    return lax.ppermute(block, axis, route)


def from_everyone(value, axis):
    copies = jnp.broadcast_to(value, (lax.axis_size(axis), *value.shape))
    return lax.all_to_all(copies, axis, split_axis=0, concat_axis=0, tiled=True)


def taken_together(value, axis):
    everything = from_everyone(value, axis)
    return jnp.sum(everything.astype(jnp.float32), axis=0)


def cut_along(value, dim, count):
    before, after = (value.shape[:dim], value.shape[dim + 1 :])
    return jnp.moveaxis(value.reshape(*before, count, -1, *after), dim, 0)


def summed_on_arrival(value, axis, dim):
    count = lax.axis_size(axis)
    pieces = lax.all_to_all(cut_along(value, dim, count), axis, 0, 0, tiled=True)
    return jnp.sum(pieces.astype(jnp.float32), axis=0)


def layer_norm(values, gain_row):
    center = values - jnp.mean(values, axis=-1, keepdims=True)
    spread = jnp.mean(center * center, axis=-1, keepdims=True)
    return center * lax.rsqrt(spread + 1e-05) * gain_row


def dense_tail(first_layer, second_weight, bias_pair, gain_row):
    hidden = jax.nn.silu(first_layer + bias_pair[0]).astype(jnp.bfloat16)
    second = jnp.dot(hidden, second_weight, preferred_element_type=jnp.float32) + bias_pair[1]
    return layer_norm(second, gain_row)


def project(node_rows, weight):
    return jnp.dot(node_rows, weight, preferred_element_type=jnp.float32)


def one_hot_sum(targets, row_count, messages):
    selector = (
        lax.broadcasted_iota(jnp.int32, (row_count, targets.shape[0]), 0) == targets[None, :]
    ).astype(jnp.bfloat16)
    return jnp.dot(selector, messages, preferred_element_type=jnp.float32)


def per_device(
    grid_nodes,
    enc_edges,
    enc_sender,
    enc_slot,
    enc_slot_node,
    mesh_nodes,
    mesh_edges,
    mesh_sender,
    mesh_receiver,
    mesh_send_node,
    grid_weights,
    enc_edge_weights,
    enc_node_weights,
    proc_edge_weights,
    proc_node_weights,
    biases,
    gains,
):
    band_index = lax.axis_index("band")
    patch_rows = mesh_nodes.shape[0]
    share_rows = patch_rows // lax.axis_size("band")
    width = mesh_nodes.shape[1]
    middle = NEIGH // 2
    slot_nodes = enc_slot_node[0]
    sender_nodes = mesh_send_node[0]
    receiver_keys = project(jnp.take(mesh_nodes, slot_nodes, axis=0), enc_edge_weights[2]).astype(
        jnp.bfloat16
    )
    receiver_keys = receiver_keys.reshape(NEIGH, CAP, width)
    key_pieces = []
    for window in range(NEIGH):
        if window == middle:
            key_pieces.append(receiver_keys[window])
        else:
            key_pieces.append(shifted(receiver_keys[window], "blk", middle - window))
    arrived_keys = jnp.concatenate(key_pieces, axis=0)
    sender_proj = project(grid_nodes, enc_edge_weights[1])
    edge_first = (
        project(enc_edges, enc_edge_weights[0])
        + jnp.take(sender_proj, enc_sender, axis=0)
        + jnp.take(arrived_keys, enc_slot, axis=0).astype(jnp.float32)
    )
    enc_message = dense_tail(edge_first, enc_edge_weights[3], biases[1], gains[1]).astype(
        jnp.bfloat16
    )
    slot_sums = one_hot_sum(enc_slot, slot_nodes.shape[0], enc_message).reshape(NEIGH, CAP, width)
    sum_pieces = []
    for window in range(NEIGH):
        if window == middle:
            sum_pieces.append(slot_sums[window])
        else:
            sum_pieces.append(
                shifted(slot_sums[window].astype(jnp.bfloat16), "blk", window - middle).astype(
                    jnp.float32
                )
            )
    landed = jnp.concatenate(sum_pieces, axis=0)
    partial_sums = jax.ops.segment_sum(landed, slot_nodes, num_segments=patch_rows)
    grid_first = project(grid_nodes, grid_weights[0])
    grid_out = (
        grid_nodes.astype(jnp.float32)
        + dense_tail(grid_first, grid_weights[1], biases[0], gains[0])
    ).astype(jnp.bfloat16)
    enc_sum = taken_together(partial_sums.astype(jnp.bfloat16), "band").astype(jnp.float32)
    node_first = project(mesh_nodes, enc_node_weights[0]) + project(
        enc_sum.astype(jnp.bfloat16), enc_node_weights[1]
    )
    mesh_mid = (
        mesh_nodes.astype(jnp.float32)
        + dense_tail(node_first, enc_node_weights[2], biases[2], gains[2])
    ).astype(jnp.bfloat16)
    target_keys = project(mesh_mid, proc_edge_weights[2]).astype(jnp.bfloat16)
    sender_rows = project(jnp.take(mesh_mid, sender_nodes, axis=0), proc_edge_weights[1]).astype(
        jnp.bfloat16
    )
    own_mid = lax.dynamic_slice_in_dim(mesh_mid, band_index * share_rows, share_rows, 0)
    arrived_senders = lax.all_to_all(sender_rows, "blk", split_axis=0, concat_axis=0, tiled=True)
    mesh_first = (
        project(mesh_edges, proc_edge_weights[0])
        + jnp.take(arrived_senders, mesh_sender, axis=0).astype(jnp.float32)
        + jnp.take(target_keys, mesh_receiver, axis=0).astype(jnp.float32)
    )
    proc_message = dense_tail(mesh_first, proc_edge_weights[3], biases[3], gains[3]).astype(
        jnp.bfloat16
    )
    receiver_sums = one_hot_sum(mesh_receiver, patch_rows, proc_message)
    proc_share = summed_on_arrival(receiver_sums.astype(jnp.bfloat16), "band", 0)
    final_first = project(own_mid, proc_node_weights[0]) + project(
        proc_share.astype(jnp.bfloat16), proc_node_weights[1]
    )
    mesh_out = (
        own_mid.astype(jnp.float32)
        + dense_tail(final_first, proc_node_weights[2], biases[4], gains[4])
    ).astype(jnp.bfloat16)
    return (grid_out, mesh_out)


def solution(mesh):
    in_specs = (
        P(("blk", "band"), None),
        P(("blk", "band"), None),
        P(("blk", "band")),
        P(("blk", "band")),
        P(("blk", "band"), None),
        P("blk", None),
        P(("blk", "band"), None),
        P(("blk", "band")),
        P(("blk", "band")),
        P(("blk", "band"), None),
        P(),
        P(),
        P(),
        P(),
        P(),
        P(),
        P(),
    )
    out_specs = (P(("blk", "band"), None), P(("blk", "band"), None))
    return jax.shard_map(
        per_device, mesh=mesh, in_specs=in_specs, out_specs=out_specs, check_vma=False
    )
```

profile of v0, /device:TPU:32, one launch (start us, length us, event | category | flops | bytes accessed | tf_op | source)
XLA Modules:
  0.0 173.5 jit_solution(16191667013547108296)
XLA Ops:
  0.6 0.0 copy-start
  0.6 0.8 compare_select_fusion.5
  1.4 0.7 compare_and_fusion.5
  2.1 0.7 compare_select_fusion.4
  2.8 3.2 %gather_fusion.2 = bf16[512,512]{1,0:T(8,128)(2,1)S(1)} fusion(bf16[640,512]{1,0:T(8,128)(2,1)} %param.26, s32[1024]{0:T(1024)S(1)} %get-tuple-element.51), kind=kCustom, calls=%fused_computation.clone | custom fusion | bytes 1050624 | tf_op jit(solution)/shard_map/jit(_take)/gather | solution.py:86
  6.0 1.6 convolution_convert_fusion.2
  7.6 3.3 %collective-permute-start = (bf16[64,512]{1,0:T(8,128)(2,1)S(1)}, bf16[64,512]{1,0:T(8,128)(2,1)S(1)}, u32[]{:S(2)}, u32[]{:S(2)}) collective-permute-start(bf16[64,512]{1,0:T(8,128)(2,1)S(1)} %get-tuple-element.22), channel_id=1, source_target_pairs={{240,0},{244,4},{248,8},{252,12},{0,16},{4,20},{8,24},{12,28},{16,... | collective-permute-start | bytes 196616 | tf_op jit(solution)/shard_map/ppermute | solution.py:13
  11.0 2.3 %collective-permute-start.1 = (bf16[64,512]{1,0:T(8,128)(2,1)S(1)}, bf16[64,512]{1,0:T(8,128)(2,1)S(1)}, u32[]{:S(2)}, u32[]{:S(2)}) collective-permute-start(bf16[64,512]{1,0:T(8,128)(2,1)S(1)} %get-tuple-element.21), channel_id=1, source_target_pairs={{244,0},{248,4},{252,8},{0,12},{4,16},{8,20},{12,24},{16,28},{20,3... | collective-permute-start | bytes 196616 | tf_op jit(solution)/shard_map/ppermute | solution.py:13
  13.3 1.0 collective-permute-start.2
  14.3 1.1 collective-permute-start.3
  15.5 1.5 fusion.44
  17.0 3.4 %collective-permute-done = bf16[64,512]{1,0:T(8,128)(2,1)S(1)} collective-permute-done((bf16[64,512]{1,0:T(8,128)(2,1)S(1)}, bf16[64,512]{1,0:T(8,128)(2,1)S(1)}, u32[]{:S(2)}, u32[]{:S(2)}) %collective-permute-start) | collective-permute-done | bytes 65568 | tf_op jit(solution)/shard_map/ppermute | solution.py:13
  20.4 0.3 collective-permute-done.1
  20.7 2.2 %collective-permute-start.4 = (bf16[64,512]{1,0:T(8,128)(2,1)S(1)}, bf16[64,512]{1,0:T(8,128)(2,1)S(1)}, u32[]{:S(2)}, u32[]{:S(2)}) collective-permute-start(bf16[64,512]{1,0:T(8,128)(2,1)S(1)} %get-tuple-element.17), channel_id=1, source_target_pairs={{4,0},{8,4},{12,8},{16,12},{20,16},{24,20},{28,24},{32,28},{36,32}... | collective-permute-start | bytes 196616 | tf_op jit(solution)/shard_map/ppermute | solution.py:13
  22.9 4.9 %gather_fusion = f32[1024,512]{1,0:T(8,128)} fusion(f32[512,512]{1,0:T(8,128)S(1)} %fusion.44, s32[1024]{0:T(1024)S(1)} %get-tuple-element.52), kind=kCustom, calls=%fused_computation.4 | custom fusion | bytes 4198400 | tf_op jit(solution)/shard_map/jit(_take)/gather | solution.py:100
  27.8 1.0 collective-permute-start.5
  28.9 2.5 %collective-permute-start.6 = (bf16[64,512]{1,0:T(8,128)(2,1)S(1)}, bf16[64,512]{1,0:T(8,128)(2,1)S(1)}, u32[]{:S(2)}, u32[]{:S(2)}) collective-permute-start(bf16[64,512]{1,0:T(8,128)(2,1)S(1)} %get-tuple-element.15), channel_id=1, source_target_pairs={{12,0},{16,4},{20,8},{24,12},{28,16},{32,20},{36,24},{40,28},{44,3... | collective-permute-start | bytes 196616 | tf_op jit(solution)/shard_map/ppermute | solution.py:13
  31.4 1.1 collective-permute-done.5
  32.4 1.0 collective-permute-done.6
  33.4 5.1 %gather_fusion.3 = bf16[1024,512]{1,0:T(8,128)(2,1)} fusion(bf16[512,512]{1,0:T(8,128)(2,1)S(1)} %constant_dynamic-update-slice_fusion, s32[1024]{0:T(1024)S(1)} %get-tuple-element.53), kind=kCustom, calls=%fused_computation.1.clone | custom fusion | bytes 2101248 | tf_op jit(solution)/shard_map/jit(_take)/gather | solution.py:101
  38.5 3.8 %add_reduce_fusion.1 = (f32[1024]{0:T(1024)S(1)}, f32[1024,512]{0,1:T(8,128)S(1)}) fusion(f32[512]{0:T(512)S(1)} %bitcast.112, bf16[4,512,512]{2,1,0:T(8,128)(2,1)} %param.32, f32[1024,512]{1,0:T(8,128)} %gather_fusion, bf16[1024,512]{1,0:T(8,128)(2,1)} %gather_fusion.3, f32[512]{0:T(512)S(1)} %bitcast.130, pred[1024]{0:T(1024)(128)(4,1)S(1)} %get-tuple-element.56, ...), kind=kOutput, calls=%fused_computation.18 | convolution fusion | flops 1080556544 | bytes 7350272 | tf_op jit(solution)/shard_map/dot_general | solution.py:45
  42.3 0.3 multiply_reduce_fusion.1
  42.7 0.9 fusion.115
  43.7 5.2 %collective-permute-start.7 = (bf16[64,512]{1,0:T(8,128)(2,1)S(1)}, bf16[64,512]{1,0:T(8,128)(2,1)S(1)}, u32[]{:S(2)}, u32[]{:S(2)}) collective-permute-start(bf16[64,512]{1,0:T(8,128)(2,1)S(1)} %get-tuple-element.14), channel_id=1, source_target_pairs={{16,0},{20,4},{24,8},{28,12},{32,16},{36,20},{40,24},{44,28},{48,3... | collective-permute-start | bytes 196616 | tf_op jit(solution)/shard_map/ppermute | solution.py:13
  48.9 1.3 collective-permute-start.8
  50.2 1.0 collective-permute-start.9
  51.2 0.5 collective-permute-start.11
  51.7 1.0 collective-permute-start.12
  52.7 3.2 %collective-permute-start.13 = (bf16[64,512]{1,0:T(8,128)(2,1)S(1)}, bf16[64,512]{1,0:T(8,128)(2,1)S(1)}, u32[]{:S(2)}, u32[]{:S(2)}) collective-permute-start(bf16[64,512]{1,0:T(8,128)(2,1)S(1)} %get-tuple-element.8), channel_id=1, source_target_pairs={{244,0},{248,4},{252,8},{0,12},{4,16},{8,20},{12,24},{16,28},{20,3... | collective-permute-start | bytes 196616 | tf_op jit(solution)/shard_map/ppermute | solution.py:13
  56.0 0.4 collective-permute-done.12
  56.5 5.8 %collective-permute-done.13 = bf16[64,512]{1,0:T(8,128)(2,1)S(1)} collective-permute-done((bf16[64,512]{1,0:T(8,128)(2,1)S(1)}, bf16[64,512]{1,0:T(8,128)(2,1)S(1)}, u32[]{:S(2)}, u32[]{:S(2)}) %collective-permute-start.13) | collective-permute-done | bytes 65568 | tf_op jit(solution)/shard_map/ppermute | solution.py:13
  62.3 4.0 %scatter_custom_fusion = f32[640,512]{1,0:T(8,128)S(1)} fusion(s32[512]{0:T(512)} %bitcast.117, f32[512,512]{1,0:T(8,128)S(1)} %convert_dynamic-update-slice_fusion, f32[]{:T(128)} %constant.60.clone.1), kind=kCustom, calls=%fused_computation.59 | custom fusion | flops 262144 | bytes 1311232 | tf_op jit(solution)/shard_map/scatter-add | solution.py:118
  66.3 0.1 convert_element_type.112
  66.4 1.7 broadcast_in_dim.64
  68.1 4.7 %all-to-all-start = ((bf16[4,640,512]{2,1,0:T(8,128)(2,1)}), bf16[4,640,512]{2,1,0:T(8,128)(2,1)}, u32[]{:S(2)}, u32[]{:S(2)}) async-start(bf16[4,640,512]{2,1,0:T(8,128)(2,1)} %broadcast_in_dim.64), calls=%async_computation | async-start | bytes 5242880 | tf_op jit(solution)/shard_map/all_to_all | solution.py:18
  72.8 1.0 copy.21
  73.8 2.3 %fusion.110 = (f32[512]{0:T(512)S(1)}, f32[512,512]{0,1:T(8,128)S(1)}) fusion(f32[512]{0:T(512)S(1)} %bitcast.127, bf16[2,512,512]{2,1,0:T(8,128)(2,1)} %param.31, bf16[512,512]{1,0:T(8,128)(2,1)S(1)} %copy-done.7, f32[512]{0:T(512)S(1)} %bitcast.128), kind=kOutput, calls=%fused_computation.172 | convolution fusion | flops 538967552 | bytes 2627584 | tf_op jit(solution)/shard_map/dot_general | solution.py:45
  76.1 3.0 %fusion.48 = f32[640,512]{1,0:T(8,128)} fusion(bf16[640,512]{1,0:T(8,128)(2,1)S(1)} %copy-done.1, bf16[3,512,512]{2,1,0:T(8,128)(2,1)} %param.33), kind=kOutput, calls=%fused_computation.76 | convolution fusion | flops 335544320 | bytes 2490368 | tf_op jit(solution)/shard_map/dot_general | solution.py:50
  79.2 23.0 %all-to-all-done = bf16[4,640,512]{2,1,0:T(8,128)(2,1)} async-done(((bf16[4,640,512]{2,1,0:T(8,128)(2,1)}), bf16[4,640,512]{2,1,0:T(8,128)(2,1)}, u32[]{:S(2)}, u32[]{:S(2)}) %all-to-all-start) | async-done | bytes 2621472 | tf_op jit(solution)/shard_map/all_to_all | solution.py:18
  102.1 2.5 %reduce_sum.118 = bf16[640,512]{1,0:T(8,128)(2,1)S(1)} reduce(bf16[4,640,512]{2,1,0:T(8,128)(2,1)} %all-to-all-done, bf16[]{:T(256)} %constant.89.clone.1), dimensions={0}, to_apply=%region_5.8 | reduce | flops 983040 | bytes 3276802 | tf_op jit(solution)/shard_map/reduce_sum | solution.py:23
  104.6 3.7 %fusion.116 = (f32[640]{0:T(1024)S(1)}, f32[640,512]{1,0:T(8,128)}) fusion(f32[512]{0:T(512)S(1)} %bitcast.125, bf16[3,512,512]{2,1,0:T(8,128)(2,1)} %param.33, f32[640,512]{1,0:T(8,128)} %fusion.48, bf16[640,512]{1,0:T(8,128)(2,1)S(1)} %reduce_sum.118, f32[512]{0:T(512)S(1)} %bitcast.126), kind=kOutput, calls=%fused_computation.174 | convolution fusion | flops 674037120 | bytes 4332032 | tf_op jit(solution)/shard_map/dot_general | solution.py:45
  108.3 1.7 multiply_reduce_fusion.2
  110.1 0.3 add_convert_fusion
  110.4 2.0 %gather_fusion.4 = bf16[512,512]{1,0:T(8,128)(2,1)S(1)} fusion(bf16[640,512]{1,0:T(8,128)(2,1)S(1)} %add_convert_fusion, s32[1024]{0:T(1024)S(1)} %get-tuple-element.50), kind=kCustom, calls=%fused_computation.2.clone | custom fusion | bytes 1050624 | tf_op jit(solution)/shard_map/jit(_take)/gather | solution.py:133
  112.4 2.4 %fusion.6 = bf16[64,8,512]{2,1,0:T(8,128)(2,1)} fusion(bf16[512,512]{1,0:T(8,128)(2,1)S(1)} %gather_fusion.4, bf16[4,512,512]{2,1,0:T(8,128)(2,1)} %param.34, pred[512]{0:T(512)(128)(4,1)S(1)} %compare_and_fusion.4), kind=kOutput, calls=%fused_computation.33 | convolution fusion | flops 268959744 | bytes 1573376 | tf_op jit(solution)/shard_map/dot_general | solution.py:50
  114.8 9.9 %all-to-all-start.1 = ((bf16[64,8,512]{2,1,0:T(8,128)(2,1)}), bf16[64,8,512]{2,1,0:T(8,128)(2,1)S(1)}, u32[]{:S(2)}, u32[]{:S(2)}) async-start(bf16[64,8,512]{2,1,0:T(8,128)(2,1)} %fusion.6), calls=%async_computation.1 | async-start | bytes 1048576 | tf_op jit(solution)/shard_map/all_to_all | solution.py:137
  124.6 0.2 multiply_reduce_fusion.3
  124.9 1.5 convolution_convert_fusion
  126.4 5.1 %gather_fusion.1 = bf16[1024,512]{1,0:T(8,128)(2,1)} fusion(bf16[640,512]{1,0:T(8,128)(2,1)S(1)} %convolution_convert_fusion, s32[1024]{0:T(1024)S(1)} %get-tuple-element.54), kind=kCustom, calls=%fused_computation.5 | custom fusion | bytes 2101248 | tf_op jit(solution)/shard_map/jit(_take)/gather | solution.py:141
  131.5 10.4 %all-to-all-done.1 = bf16[64,8,512]{2,1,0:T(8,128)(2,1)S(1)} async-done(((bf16[64,8,512]{2,1,0:T(8,128)(2,1)}), bf16[64,8,512]{2,1,0:T(8,128)(2,1)S(1)}, u32[]{:S(2)}, u32[]{:S(2)}) %all-to-all-start.1) | async-done | bytes 524320 | tf_op jit(solution)/shard_map/all_to_all | solution.py:137
  141.8 5.1 %gather_fusion.5 = bf16[1024,512]{1,0:T(8,128)(2,1)} fusion(bf16[512,512]{1,0:T(8,128)(2,1)S(1)} %bitcast.105, s32[1024]{0:T(1024)S(1)} %get-tuple-element.55), kind=kCustom, calls=%fused_computation.3.clone | custom fusion | bytes 2101248 | tf_op jit(solution)/shard_map/jit(_take)/gather | solution.py:140
  146.9 4.8 %add_reduce_fusion = (f32[1024]{0:T(1024)S(1)}, f32[1024,512]{0,1:T(8,128)}) fusion(f32[512]{0:T(512)S(1)} %bitcast.109, bf16[4,512,512]{2,1,0:T(8,128)(2,1)} %param.34, bf16[1024,512]{1,0:T(8,128)(2,1)} %param.27, bf16[1024,512]{1,0:T(8,128)(2,1)} %gather_fusion.5, f32[512]{0:T(512)S(1)} %bitcast.124, bf16[1024,512]{1,0:T(8,128)(2,1)S(1)} %copy-done.8, ...), kind=kOutput, calls=%fused_computation.17 | convolution fusion | flops 1081080832 | bytes 6301696 | tf_op jit(solution)/shard_map/dot_general | solution.py:45
  151.7 2.1 %multiply_reduce_fusion = f32[1024]{0:T(1024)S(1)} fusion(f32[1024,512]{0,1:T(8,128)} %get-tuple-element.47, f32[1024]{0:T(1024)S(1)} %broadcast_multiply_fusion.1, f32[512]{0:T(512)S(1)} %bitcast.110), kind=kLoop, calls=%fused_computation.10 | loop fusion | flops 2096128 | bytes 2107392 | tf_op jit(solution)/shard_map/reduce_sum | solution.py:39
  153.8 0.1 copy-done.5
  153.9 1.9 %fusion.3 = bf16[640,512]{1,0:T(8,128)(2,1)} fusion(s32[1024]{0:T(1024)S(1)} %copy-done.13, f32[1024,512]{0,1:T(8,128)S(1)} %copy-done.5, f32[512]{0:T(512)S(1)} %bitcast.123, f32[1024]{0:T(1024)S(1)} %add_rsqrt_fusion, f32[1024]{0:T(1024)S(1)} %broadcast_multiply_fusion.1, f32[512]{0:T(512)S(1)} %bitcast.111), kind=kOutput, calls=%fused_computation.24 | convolution fusion | flops 674693120 | bytes 2768896 | tf_op jit(solution)/shard_map/dot_general | solution.py:57
  155.9 3.5 %all-to-all-start.2 = ((bf16[4,160,512]{2,1,0:T(8,128)(2,1)}), bf16[4,160,512]{2,1,0:T(8,128)(2,1)S(1)}, u32[]{:S(2)}, u32[]{:S(2)}) async-start(bf16[4,160,512]{2,1,0:T(8,128)(2,1)} %bitcast.106), calls=%async_computation.2 | async-start | bytes 1310720 | tf_op jit(solution)/shard_map/all_to_all | solution.py:33
  159.4 2.0 %add_convert_fusion.1 = bf16[512,512]{0,1:T(8,128)(2,1)} fusion(bf16[512,512]{0,1:T(8,128)(2,1)} %copy.21, f32[512,512]{0,1:T(8,128)S(1)} %copy-done.4, f32[512]{0:T(512)S(1)} %bitcast.108, f32[512]{0:T(512)S(1)} %add_rsqrt_fusion.3, f32[512]{0:T(512)S(1)} %broadcast_multiply_fusion.3), kind=kLoop, calls=%fused_computation.50 | loop fusion | flops 1572864 | bytes 2103296 | tf_op jit(solution)/shard_map/convert_element_type | solution.py:123
  161.4 2.0 %copy.22 = bf16[512,512]{1,0:T(8,128)(2,1)} copy(bf16[512,512]{0,1:T(8,128)(2,1)} %add_convert_fusion.1) | data formatting | bytes 1048576
  163.5 1.3 fusion.37
  164.8 5.7 %all-to-all-done.2 = bf16[4,160,512]{2,1,0:T(8,128)(2,1)S(1)} async-done(((bf16[4,160,512]{2,1,0:T(8,128)(2,1)}), bf16[4,160,512]{2,1,0:T(8,128)(2,1)S(1)}, u32[]{:S(2)}, u32[]{:S(2)}) %all-to-all-start.2) | async-done | bytes 655392 | tf_op jit(solution)/shard_map/all_to_all | solution.py:33
  170.5 0.1 reduce_sum.123
  170.6 1.8 %fusion.121 = (f32[160]{0:T(256)S(1)}, f32[160,512]{1,0:T(8,128)S(1)}) fusion(f32[512]{0:T(512)S(1)} %bitcast.122, bf16[3,512,512]{2,1,0:T(8,128)(2,1)} %param.35, f32[160,512]{1,0:T(8,128)S(1)} %fusion.37, bf16[160,512]{1,0:T(8,128)(2,1)S(1)} %reduce_sum.123, f32[512]{0:T(512)S(1)} %bitcast.121), kind=kOutput, calls=%fused_computation.175 | convolution fusion | flops 168509280 | bytes 1872512 | tf_op jit(solution)/shard_map/dot_general | solution.py:45
  172.4 0.2 multiply_reduce_fusion.4
  172.6 0.8 add_convert_fusion.2
  (75 shorter events, 0.4 us)
Async XLA Ops:
  0.6 37.8 %copy-start = (bf16[1024,512]{1,0:T(8,128)(2,1)S(1)}, bf16[1024,512]{1,0:T(8,128)(2,1)}, u32[]{:S(2)}) copy-start(bf16[1024,512]{1,0:T(8,128)(2,1)} %param.22) | copy-start | bytes 3145732
  6.0 9.5 %copy-start.9 = (f32[5,2,512]{2,1,0:T(2,128)S(1)}, f32[5,2,512]{2,1,0:T(2,128)}, u32[]{:S(2)}) copy-start(f32[5,2,512]{2,1,0:T(2,128)} %param.36) | copy-start | bytes 61444
  6.0 9.5 %copy-start.6 = (bf16[512,512]{1,0:T(8,128)(2,1)S(1)}, bf16[512,512]{1,0:T(8,128)(2,1)}, u32[]{:S(2)}) copy-start(bf16[512,512]{1,0:T(8,128)(2,1)} %param.21) | copy-start | bytes 1572868
  6.0 11.0 %copy-start.15 = (f32[5,512]{1,0:T(8,128)S(1)}, f32[5,512]{1,0:T(8,128)}, u32[]{:S(2)}) copy-start(f32[5,512]{1,0:T(8,128)} %param.37) | copy-start | bytes 30724
  6.0 11.0 %copy-start.10 = (s32[1024]{0:T(1024)S(1)}, s32[1024]{0:T(1024)}, u32[]{:S(2)}) copy-start(s32[1024]{0:T(1024)} %param.23) | copy-start | bytes 12292
  6.0 11.0 %copy-start.11 = (s32[1024]{0:T(1024)S(1)}, s32[1024]{0:T(1024)}, u32[]{:S(2)}) copy-start(s32[1024]{0:T(1024)} %param.24) | copy-start | bytes 12292
  7.6 12.7 %collective-permute-start = (bf16[64,512]{1,0:T(8,128)(2,1)S(1)}, bf16[64,512]{1,0:T(8,128)(2,1)S(1)}, u32[]{:S(2)}, u32[]{:S(2)}) collective-permute-start(bf16[64,512]{1,0:T(8,128)(2,1)S(1)} %get-tuple-element.22), channel_id=1, source_target_pairs={{240,0},{244,4},{248,8},{252,12},{0,16},{4,20},{8,24},{12,28},{16,... | collective-permute-start | bytes 196616 | tf_op jit(solution)/shard_map/ppermute | solution.py:13
  11.0 9.7 %collective-permute-start.1 = (bf16[64,512]{1,0:T(8,128)(2,1)S(1)}, bf16[64,512]{1,0:T(8,128)(2,1)S(1)}, u32[]{:S(2)}, u32[]{:S(2)}) collective-permute-start(bf16[64,512]{1,0:T(8,128)(2,1)S(1)} %get-tuple-element.21), channel_id=1, source_target_pairs={{244,0},{248,4},{252,8},{0,12},{4,16},{8,20},{12,24},{16,28},{20,3... | collective-permute-start | bytes 196616 | tf_op jit(solution)/shard_map/ppermute | solution.py:13
  13.3 7.4 %collective-permute-start.2 = (bf16[64,512]{1,0:T(8,128)(2,1)S(1)}, bf16[64,512]{1,0:T(8,128)(2,1)S(1)}, u32[]{:S(2)}, u32[]{:S(2)}) collective-permute-start(bf16[64,512]{1,0:T(8,128)(2,1)S(1)} %get-tuple-element.20), channel_id=1, source_target_pairs={{248,0},{252,4},{0,8},{4,12},{8,16},{12,20},{16,24},{20,28},{24,32... | collective-permute-start | bytes 196616 | tf_op jit(solution)/shard_map/ppermute | solution.py:13
  14.3 6.4 %collective-permute-start.3 = (bf16[64,512]{1,0:T(8,128)(2,1)S(1)}, bf16[64,512]{1,0:T(8,128)(2,1)S(1)}, u32[]{:S(2)}, u32[]{:S(2)}) collective-permute-start(bf16[64,512]{1,0:T(8,128)(2,1)S(1)} %get-tuple-element.19), channel_id=1, source_target_pairs={{252,0},{0,4},{4,8},{8,12},{12,16},{16,20},{20,24},{24,28},{28,32}... | collective-permute-start | bytes 196616 | tf_op jit(solution)/shard_map/ppermute | solution.py:13
  20.7 10.6 %collective-permute-start.4 = (bf16[64,512]{1,0:T(8,128)(2,1)S(1)}, bf16[64,512]{1,0:T(8,128)(2,1)S(1)}, u32[]{:S(2)}, u32[]{:S(2)}) collective-permute-start(bf16[64,512]{1,0:T(8,128)(2,1)S(1)} %get-tuple-element.17), channel_id=1, source_target_pairs={{4,0},{8,4},{12,8},{16,12},{20,16},{24,20},{28,24},{32,28},{36,32}... | collective-permute-start | bytes 196616 | tf_op jit(solution)/shard_map/ppermute | solution.py:13
  27.8 4.6 %collective-permute-start.5 = (bf16[64,512]{1,0:T(8,128)(2,1)S(1)}, bf16[64,512]{1,0:T(8,128)(2,1)S(1)}, u32[]{:S(2)}, u32[]{:S(2)}) collective-permute-start(bf16[64,512]{1,0:T(8,128)(2,1)S(1)} %get-tuple-element.16), channel_id=1, source_target_pairs={{8,0},{12,4},{16,8},{20,12},{24,16},{28,20},{32,24},{36,28},{40,32... | collective-permute-start | bytes 196616 | tf_op jit(solution)/shard_map/ppermute | solution.py:13
  28.9 4.5 %collective-permute-start.6 = (bf16[64,512]{1,0:T(8,128)(2,1)S(1)}, bf16[64,512]{1,0:T(8,128)(2,1)S(1)}, u32[]{:S(2)}, u32[]{:S(2)}) collective-permute-start(bf16[64,512]{1,0:T(8,128)(2,1)S(1)} %get-tuple-element.15), channel_id=1, source_target_pairs={{12,0},{16,4},{20,8},{24,12},{28,16},{32,20},{36,24},{40,28},{44,3... | collective-permute-start | bytes 196616 | tf_op jit(solution)/shard_map/ppermute | solution.py:13
  43.7 8.0 %collective-permute-start.7 = (bf16[64,512]{1,0:T(8,128)(2,1)S(1)}, bf16[64,512]{1,0:T(8,128)(2,1)S(1)}, u32[]{:S(2)}, u32[]{:S(2)}) collective-permute-start(bf16[64,512]{1,0:T(8,128)(2,1)S(1)} %get-tuple-element.14), channel_id=1, source_target_pairs={{16,0},{20,4},{24,8},{28,12},{32,16},{36,20},{40,24},{44,28},{48,3... | collective-permute-start | bytes 196616 | tf_op jit(solution)/shard_map/ppermute | solution.py:13
  48.9 3.9 %collective-permute-start.8 = (bf16[64,512]{1,0:T(8,128)(2,1)S(1)}, bf16[64,512]{1,0:T(8,128)(2,1)S(1)}, u32[]{:S(2)}, u32[]{:S(2)}) collective-permute-start(bf16[64,512]{1,0:T(8,128)(2,1)S(1)} %get-tuple-element.13), channel_id=1, source_target_pairs={{12,0},{16,4},{20,8},{24,12},{28,16},{32,20},{36,24},{40,28},{44,3... | collective-permute-start | bytes 196616 | tf_op jit(solution)/shard_map/ppermute | solution.py:13
  50.2 5.7 %collective-permute-start.9 = (bf16[64,512]{1,0:T(8,128)(2,1)S(1)}, bf16[64,512]{1,0:T(8,128)(2,1)S(1)}, u32[]{:S(2)}, u32[]{:S(2)}) collective-permute-start(bf16[64,512]{1,0:T(8,128)(2,1)S(1)} %get-tuple-element.12), channel_id=1, source_target_pairs={{8,0},{12,4},{16,8},{20,12},{24,16},{28,20},{32,24},{36,28},{40,32... | collective-permute-start | bytes 196616 | tf_op jit(solution)/shard_map/ppermute | solution.py:13
  51.2 4.8 %collective-permute-start.10 = (bf16[64,512]{1,0:T(8,128)(2,1)S(1)}, bf16[64,512]{1,0:T(8,128)(2,1)S(1)}, u32[]{:S(2)}, u32[]{:S(2)}) collective-permute-start(bf16[64,512]{1,0:T(8,128)(2,1)S(1)} %get-tuple-element.11), channel_id=1, source_target_pairs={{4,0},{8,4},{12,8},{16,12},{20,16},{24,20},{28,24},{32,28},{36,32}... | collective-permute-start | bytes 196616 | tf_op jit(solution)/shard_map/ppermute | solution.py:13
  51.2 4.8 %collective-permute-start.11 = (bf16[64,512]{1,0:T(8,128)(2,1)S(1)}, bf16[64,512]{1,0:T(8,128)(2,1)S(1)}, u32[]{:S(2)}, u32[]{:S(2)}) collective-permute-start(bf16[64,512]{1,0:T(8,128)(2,1)S(1)} %get-tuple-element.10), channel_id=1, source_target_pairs={{252,0},{0,4},{4,8},{8,12},{12,16},{16,20},{20,24},{24,28},{28,32}... | collective-permute-start | bytes 196616 | tf_op jit(solution)/shard_map/ppermute | solution.py:13
  51.7 4.8 %collective-permute-start.12 = (bf16[64,512]{1,0:T(8,128)(2,1)S(1)}, bf16[64,512]{1,0:T(8,128)(2,1)S(1)}, u32[]{:S(2)}, u32[]{:S(2)}) collective-permute-start(bf16[64,512]{1,0:T(8,128)(2,1)S(1)} %get-tuple-element.9), channel_id=1, source_target_pairs={{248,0},{252,4},{0,8},{4,12},{8,16},{12,20},{16,24},{20,28},{24,32... | collective-permute-start | bytes 196616 | tf_op jit(solution)/shard_map/ppermute | solution.py:13
  52.7 9.5 %collective-permute-start.13 = (bf16[64,512]{1,0:T(8,128)(2,1)S(1)}, bf16[64,512]{1,0:T(8,128)(2,1)S(1)}, u32[]{:S(2)}, u32[]{:S(2)}) collective-permute-start(bf16[64,512]{1,0:T(8,128)(2,1)S(1)} %get-tuple-element.8), channel_id=1, source_target_pairs={{244,0},{248,4},{252,8},{0,12},{4,16},{8,20},{12,24},{16,28},{20,3... | collective-permute-start | bytes 196616 | tf_op jit(solution)/shard_map/ppermute | solution.py:13
  68.1 4.7 %copy-start.7 = (bf16[512,512]{1,0:T(8,128)(2,1)S(1)}, bf16[512,512]{1,0:T(8,128)(2,1)}, u32[]{:S(2)}) copy-start(bf16[512,512]{1,0:T(8,128)(2,1)} %param.21) | copy-start | bytes 1572868
  68.1 5.7 %copy-start.14 = (s32[1,512]{1,0:T(1,128)S(1)}, s32[1,512]{1,0:T(1,128)}, u32[]{:S(2)}) copy-start(s32[1,512]{1,0:T(1,128)} %param.30) | copy-start | bytes 6148
  68.1 34.0 %all-to-all-start = ((bf16[4,640,512]{2,1,0:T(8,128)(2,1)}), bf16[4,640,512]{2,1,0:T(8,128)(2,1)}, u32[]{:S(2)}, u32[]{:S(2)}) async-start(bf16[4,640,512]{2,1,0:T(8,128)(2,1)} %broadcast_in_dim.64), calls=%async_computation | async-start | bytes 5242880 | tf_op jit(solution)/shard_map/all_to_all | solution.py:18
  73.8 2.3 %copy-start.1 = (bf16[640,512]{1,0:T(8,128)(2,1)S(1)}, bf16[640,512]{1,0:T(8,128)(2,1)}, u32[]{:S(2)}) copy-start(bf16[640,512]{1,0:T(8,128)(2,1)} %param.26) | copy-start | bytes 1966084
  76.1 48.5 %copy-start.3 = (f32[512,512]{0,1:T(8,128)}, f32[512,512]{0,1:T(8,128)S(1)}, u32[]{:S(2)}) copy-start(f32[512,512]{0,1:T(8,128)S(1)} %get-tuple-element.39) | copy-start | bytes 3145732
  108.3 1.7 copy-start.2
  112.4 12.5 %copy-start.12 = (s32[1024]{0:T(1024)S(1)}, s32[1024]{0:T(1024)}, u32[]{:S(2)}) copy-start(s32[1024]{0:T(1024)} %param.28) | copy-start | bytes 12292
  112.4 12.5 %copy-start.13 = (s32[1024]{0:T(1024)S(1)}, s32[1024]{0:T(1024)}, u32[]{:S(2)}) copy-start(s32[1024]{0:T(1024)} %param.29) | copy-start | bytes 12292
  114.8 27.1 %all-to-all-start.1 = ((bf16[64,8,512]{2,1,0:T(8,128)(2,1)}), bf16[64,8,512]{2,1,0:T(8,128)(2,1)S(1)}, u32[]{:S(2)}, u32[]{:S(2)}) async-start(bf16[64,8,512]{2,1,0:T(8,128)(2,1)} %fusion.6), calls=%async_computation.1 | async-start | bytes 1048576 | tf_op jit(solution)/shard_map/all_to_all | solution.py:137
  141.8 5.1 %copy-start.8 = (bf16[1024,512]{1,0:T(8,128)(2,1)S(1)}, bf16[1024,512]{1,0:T(8,128)(2,1)}, u32[]{:S(2)}) copy-start(bf16[1024,512]{1,0:T(8,128)(2,1)} %gather_fusion.1) | copy-start | bytes 3145732
  151.7 2.2 %copy-start.5 = (f32[1024,512]{0,1:T(8,128)S(1)}, f32[1024,512]{0,1:T(8,128)}, u32[]{:S(2)}) copy-start(f32[1024,512]{0,1:T(8,128)} %get-tuple-element.47) | copy-start | bytes 6291460
  153.9 5.4 %copy-start.4 = (f32[512,512]{0,1:T(8,128)S(1)}, f32[512,512]{0,1:T(8,128)}, u32[]{:S(2)}) copy-start(f32[512,512]{0,1:T(8,128)} %copy-done.3) | copy-start | bytes 3145732
  155.9 14.6 %all-to-all-start.2 = ((bf16[4,160,512]{2,1,0:T(8,128)(2,1)}), bf16[4,160,512]{2,1,0:T(8,128)(2,1)S(1)}, u32[]{:S(2)}, u32[]{:S(2)}) async-start(bf16[4,160,512]{2,1,0:T(8,128)(2,1)} %bitcast.106), calls=%async_computation.2 | async-start | bytes 1310720 | tf_op jit(solution)/shard_map/all_to_all | solution.py:33
where the time goes:
time: 175 us; the launch traced here: 173 us
  waiting for transfers between devices  51 us (29%)
  starting transfers between devices  43.7 us (25%)
  matrix products  30.6 us (17%)
  local copies, waits for them, and re-layouts  30.3 us (17%)
  other arithmetic  16.7 us (10%)
    ppermute x14, starting transfers between devices, shifted(): return lax.ppermute(block, axis, route)  25.7 us
    all_to_all x1, waiting for transfers between devices, from_everyone(): return lax.all_to_all(copies, axis, split_axis=0, concat_axis=0, tiled=True)  23 us
    dot_general x5, matrix products, dense_tail(): jnp.dot(hidden, second_weight, preferred_element_type=jnp.float32)  16.4 us
    ppermute x14, waiting for transfers between devices, shifted(): return lax.ppermute(block, axis, route)  11.9 us
    dot_general x6, matrix products, project(): return jnp.dot(node_rows, weight, preferred_element_type=jnp.float32)  11.3 us
    all_to_all x1, waiting for transfers between devices, per_device(): lax.all_to_all(sender_rows, 'blk', split_axis=0, concat_axis=0, tiled=True)  10.4 us
    all_to_all x1, starting transfers between devices, per_device(): lax.all_to_all(sender_rows, 'blk', split_axis=0, concat_axis=0, tiled=True)  9.86 us
    all_to_all x1, waiting for transfers between devices, summed_on_arrival(): lax.all_to_all(cut_along(value, dim, count), axis, 0, 0, tiled=True)  5.75 us
  transfers between devices with their start and end apart: 17, of which 9 were waited for; matrix products, arithmetic and copies ran while one was open for 14% of the time, Pallas kernels for 0%

commit v1 on v0

v1 whole, which is shorter than its diff:
```python
import jax
import jax.numpy as jnp
from jax import lax
from jax.experimental import pallas as pl
from jax.experimental.pallas import tpu as pltpu
from jax.sharding import PartitionSpec as P

NEIGH = 8
CAP = 64
MIDDLE = NEIGH // 2
WINDOWS = [k for k in range(NEIGH) if k != MIDDLE]
NC = 2
MESH = pl.DeviceIdType.MESH
BF = jnp.bfloat16
F32 = jnp.float32
LANES = 128


def dot(a, b):
    return jnp.dot(a, b, preferred_element_type=F32)


def silu(v):
    half = 0.5 * v
    return half + half * jnp.tanh(half)


def norm(values, gain_row):
    center = values - jnp.mean(values, axis=-1, keepdims=True)
    spread = jnp.mean(center * center, axis=-1, keepdims=True)
    return center * lax.rsqrt(spread + 1e-05) * gain_row


def one_hot(flags):
    return jnp.where(flags, 1.0, 0.0).astype(BF)


def down_column(row):
    return jnp.transpose(jnp.broadcast_to(row, (LANES, LANES)))


def rows_select(column, width, start=0):
    lane = lax.broadcasted_iota(jnp.int32, (LANES, LANES), 1)
    return jnp.concatenate(
        [one_hot(column == lane + (start + j)) for j in range(0, width, LANES)], axis=1
    )


def cols_select(row, height):
    return one_hot(lax.broadcasted_iota(jnp.int32, (height, LANES), 0) == row)


def kernel(
    grid_nodes, enc_edges, enc_sender, enc_slot, enc_slot_node, mesh_nodes, mesh_edges,
    mesh_sender, mesh_receiver, mesh_send_node, grid_w, enc_w, node_w, proc_w, final_w,
    biases, gains,
    grid_out, mesh_out,
    v_grid, v_ee, v_esnd, v_eslot, v_esn, v_mesh, v_me, v_msnd, v_mrcv, v_msn,
    v_gw, v_ew, v_nw, v_pw, v_fw, v_bias, v_gain, v_go, v_mo,
    keys, arrived, ssum, landed, part, far, near, relay, relayed, mid, srows, arr, arr2,
    part2, far2, near2, relay2, relayed2,
    g_key, g_slot, s_slot, g_snd, p_node, g_send, g_msnd, g_rcv, r_rcv,
    sproj, acc, acc2, opart, msg, base_mid, base_fin, gsel, tkeys,
    load_sem, out_sem, ka_s, ka_r, cs_s, cs_r, rs_s, rs_r, ag_s, ag_r, aa_s, aa_r, rt_s, rt_r,
):
    n_blk = lax.axis_size("blk")
    n_band = lax.axis_size("band")
    blk = lax.axis_index("blk")
    band = lax.axis_index("band")
    left = lax.rem(band + n_band - 1, n_band)
    right = lax.rem(band + 1, n_band)
    across = lax.rem(band + 2, n_band)
    width = v_mesh.shape[1]
    wc = width // NC
    nodes = v_mesh.shape[0]
    share = nodes // n_band
    slots = NEIGH * CAP
    edges = v_ee.shape[0]
    medges = v_me.shape[0]
    cols = [slice(c * wc, (c + 1) * wc) for c in range(NC)]

    loads = {}

    def load(name, src, dst):
        copy = pltpu.make_async_copy(src, dst, load_sem.at[len(loads)])
        copy.start()
        loads[name] = copy

    def ready(*names):
        for name in names:
            loads[name].wait()

    load("esn", enc_slot_node, v_esn)
    load("mesh", mesh_nodes, v_mesh)
    load("ew2", enc_w.at[2], v_ew.at[2])

    barrier = pltpu.get_barrier_semaphore()

    @pl.loop(1, n_blk)
    def _(r):
        pl.semaphore_signal(
            barrier, inc=1, device_id=(lax.rem(blk + r, n_blk), band), device_id_type=MESH
        )

    for peer in (left, right):
        pl.semaphore_signal(barrier, inc=1, device_id=(blk, peer), device_id_type=MESH)

    load("grid", grid_nodes, v_grid)
    load("ew1", enc_w.at[1], v_ew.at[1])
    load("esnd", enc_sender, v_esnd)
    load("eslot", enc_slot, v_eslot)
    load("bias", biases, v_bias)
    load("gain", gains, v_gain)
    load("ee", enc_edges, v_ee)
    load("ew0", enc_w.at[0], v_ew.at[0])
    load("ew3", enc_w.at[3], v_ew.at[3])
    load("nw0", node_w.at[0], v_nw.at[0])
    load("nw1", node_w.at[1], v_nw.at[1])
    load("nw2", node_w.at[2], v_nw.at[2])
    load("msn", mesh_send_node, v_msn)
    load("msnd", mesh_sender, v_msnd)
    load("mrcv", mesh_receiver, v_mrcv)
    load("me", mesh_edges, v_me)
    load("pw", proc_w, v_pw)
    load("gw", grid_w, v_gw)
    load("fw", final_w, v_fw)

    def remote(src, dst, send, recv, to_blk, to_band):
        return pltpu.make_async_remote_copy(
            src_ref=src, dst_ref=dst, send_sem=send, recv_sem=recv,
            device_id=(to_blk, to_band), device_id_type=MESH,
        )

    sent = []

    ready("esn")
    for r in range(slots // LANES):
        column = down_column(v_esn[0:1, r * LANES : (r + 1) * LANES])
        g_key[r * LANES : (r + 1) * LANES, :] = rows_select(column, nodes)
    ready("mesh", "ew2")
    gsel[...] = dot(g_key[...], v_mesh[...]).astype(BF)
    key_copies = []
    for c in range(NC):
        projected = dot(gsel[...], v_ew[2, :, cols[c]]).astype(BF)
        keys[c] = projected.reshape(NEIGH, CAP, wc)
        if c == 0:
            pl.semaphore_wait(barrier, n_blk - 1 + 2)
        copies = []
        for i, k in enumerate(WINDOWS):
            copy = remote(
                keys.at[c, k], arrived.at[c, k], ka_s.at[c, i], ka_r.at[c, i],
                lax.rem(blk + MIDDLE - k + n_blk, n_blk), band,
            )
            copy.start()
            copies.append(copy)
        key_copies.append(copies)
        sent += copies
        arrived[c, MIDDLE] = keys[c, MIDDLE]

    ready("grid", "ew1")
    sproj[...] = dot(v_grid[...], v_ew[1]).astype(BF)
    ready("esnd", "eslot")

    @pl.loop(0, edges // LANES)
    def _(r):
        rows = pl.ds(pl.multiple_of(r * LANES, LANES), LANES)
        g_snd[rows, :] = rows_select(down_column(v_esnd[pl.ds(r, 1), :]), v_grid.shape[0])
        slot_row = v_eslot[pl.ds(r, 1), :]
        g_slot[rows, :] = rows_select(down_column(slot_row), slots)
        s_slot[:, rows] = cols_select(slot_row, slots)

    ready("bias", "gain", "ee", "ew0")
    TILE = 256

    @pl.loop(0, edges // TILE)
    def _(t):
        rows = pl.ds(pl.multiple_of(t * TILE, TILE), TILE)
        acc[rows, :] = (
            dot(v_ee[rows, :], v_ew[0]) + dot(g_snd[rows, :], sproj[...]) + v_bias[1, 0:1, :]
        )

    ready("ew3")

    for c in range(NC):
        for copy in key_copies[c]:
            copy.wait_recv()

        @pl.loop(0, edges // TILE)
        def _(t):
            rows = pl.ds(pl.multiple_of(t * TILE, TILE), TILE)
            first = acc[rows, cols[c]] + dot(g_slot[rows, :], arrived[c].reshape(slots, wc))
            second = dot(silu(first).astype(BF), v_ew[3, cols[c], :])
            if c > 0:
                second = second + opart[rows, :]
            if c < NC - 1:
                opart[rows, :] = second
            else:
                msg[rows, :] = norm(second + v_bias[1, 1:2, :], v_gain[1:2, :]).astype(BF)

    sum_copies = []
    for c in range(NC):
        ssum[c] = dot(s_slot[...], msg[:, cols[c]]).astype(BF).reshape(NEIGH, CAP, wc)
        copies = []
        for i, k in enumerate(WINDOWS):
            copy = remote(
                ssum.at[c, k], landed.at[c, k], cs_s.at[c, i], cs_r.at[c, i],
                lax.rem(blk + k - MIDDLE + n_blk, n_blk), band,
            )
            copy.start()
            copies.append(copy)
        sum_copies.append(copies)
        sent += copies
        landed[c, MIDDLE] = ssum[c, MIDDLE]

    for r in range(slots // LANES):
        select = cols_select(v_esn[0:1, r * LANES : (r + 1) * LANES], nodes)
        p_node[:, :, r * LANES : (r + 1) * LANES] = select.reshape(n_band, share, LANES)
    ready("nw0", "nw1", "nw2", "msn", "msnd", "mrcv")
    own_rows = pl.ds(pl.multiple_of(band * share, 32), share)
    base_mid[...] = dot(v_mesh[own_rows, :], v_nw[0]) + v_bias[2, 0:1, :]
    for r in range(v_msn.shape[1] // LANES):
        column = down_column(v_msn[0:1, r * LANES : (r + 1) * LANES])
        g_send[r * LANES : (r + 1) * LANES, :] = rows_select(column, nodes)

    def toward(c):
        return (left, right) if c == 0 else (right, left)

    def scatter_start(c, part, far, near, sem_s, sem_r):
        first, other = toward(c)
        far_copy = remote(part.at[c, across], far.at[c], sem_s.at[c, 0], sem_r.at[c, 0], blk, first)
        near_copy = remote(part.at[c, other], near.at[c], sem_s.at[c, 1], sem_r.at[c, 1], blk, other)
        far_copy.start()
        near_copy.start()
        return far_copy, near_copy

    def scatter_relay(c, far_copy, part, far, relay, relayed, sem_s, sem_r):
        first, _ = toward(c)
        far_copy.wait_recv()
        relay[c] = (far[c].astype(F32) + part[c, first].astype(F32)).astype(BF)
        copy = remote(relay.at[c], relayed.at[c], sem_s.at[c, 2], sem_r.at[c, 2], blk, first)
        copy.start()
        return copy

    scatters = []
    for c in range(NC):
        for copy in sum_copies[c]:
            copy.wait_recv()
        sums = landed[c].reshape(slots, wc)
        for s in range(n_band):
            part[c, s] = dot(p_node[s], sums).astype(BF)
        scatters.append(scatter_start(c, part, far, near, rs_s, rs_r))
    relays = []
    for c in range(NC):
        relays.append(scatter_relay(c, scatters[c][0], part, far, relay, relayed, rs_s, rs_r))
        sent += [*scatters[c], relays[c]]

    first = base_mid[...]
    for c in range(NC):
        scatters[c][1].wait_recv()
        relays[c].wait_recv()
        total = part[c, band].astype(F32) + near[c].astype(F32) + relayed[c].astype(F32)
        first = first + dot(total.astype(BF), v_nw[1, cols[c], :])
    tail = norm(dot(silu(first).astype(BF), v_nw[2]) + v_bias[2, 1:2, :], v_gain[2:3, :])
    own_mid = (v_mesh[own_rows, :].astype(F32) + tail).astype(BF)
    for c in range(NC):
        mid[c, band] = own_mid[:, cols[c]]

    gathers = {}
    for c in range(NC):
        first_peer, other_peer = toward(c)
        for hop, peer in ((0, first_peer), (1, other_peer)):
            gathers[c, hop] = remote(
                mid.at[c, band], mid.at[c, band], ag_s.at[c, hop], ag_r.at[c, hop], blk, peer
            )
    for hop in range(2):
        for c in range(NC):
            gathers[c, hop].start()

    ready("me", "pw")

    @pl.loop(0, medges // LANES)
    def _(r):
        rows = pl.ds(pl.multiple_of(r * LANES, LANES), LANES)
        acc2[rows, :] = dot(v_me[rows, :], v_pw[0]) + v_bias[3, 0:1, :]
        g_msnd[rows, :] = rows_select(down_column(v_msnd[pl.ds(r, 1), :]), slots)

    for c in range(NC):
        first_peer, other_peer = toward(c)
        gathers[c, 0].wait_recv()
        gathers[c, 2] = remote(
            mid.at[c, other_peer], mid.at[c, other_peer], ag_s.at[c, 2], ag_r.at[c, 2], blk, first_peer
        )
        gathers[c, 2].start()
    base_fin[...] = v_bias[4, 0:1, :] + jnp.zeros_like(base_fin)
    requested = None
    for c in range(NC):
        gathers[c, 1].wait_recv()
        gathers[c, 2].wait_recv()
        picked = dot(g_send[...], mid[c].reshape(nodes, wc)).astype(BF)
        term = dot(picked, v_pw[1, cols[c], :])
        requested = term if requested is None else requested + term
    sent += list(gathers.values())
    srows[...] = requested.reshape(srows.shape).astype(BF)

    @pl.loop(0, n_blk - 1)
    def _(i):
        step = (i + 1) // 2
        r = n_blk // 2 + step * (1 - 2 * lax.rem(i, 2))
        to = lax.rem(blk + r, n_blk)
        remote(srows.at[to], arr.at[blk], aa_s, aa_r, to, band).start()

    arr[blk] = srows[blk]

    tk = None
    for c in range(NC):
        term = dot(mid[c].reshape(nodes, wc), v_pw[2, cols[c], :])
        tk = term if tk is None else tk + term
    tkeys[...] = tk.astype(BF)

    @pl.loop(0, medges // LANES)
    def _(r):
        rows = pl.ds(pl.multiple_of(r * LANES, LANES), LANES)
        receiver_row = v_mrcv[pl.ds(r, 1), :]
        select = rows_select(down_column(receiver_row), nodes)
        acc2[rows, :] = acc2[rows, :] + dot(select, tkeys[...])
        r_rcv[:, rows] = cols_select(receiver_row, nodes)

    ready("gw")

    @pl.loop(0, v_grid.shape[0] // TILE)
    def _(t):
        rows = pl.ds(pl.multiple_of(t * TILE, TILE), TILE)
        first = dot(v_grid[rows, :], v_gw[0]) + v_bias[0, 0:1, :]
        tail = norm(dot(silu(first).astype(BF), v_gw[1]) + v_bias[0, 1:2, :], v_gain[0:1, :])
        v_go[rows, :] = (v_grid[rows, :].astype(F32) + tail).astype(BF)

    grid_copy = pltpu.make_async_copy(v_go, grid_out, out_sem.at[0])
    grid_copy.start()
    ready("fw")
    fin = v_bias[4, 0:1, :]
    for c in range(NC):
        fin = fin + dot(mid[c, band], v_fw[0, cols[c], :])
    base_fin[...] = fin

    blocks = pl.ds(0, n_blk - 1)
    everyone = remote(srows.at[blocks], arr.at[blocks], aa_s, aa_r, blk, band)
    everyone.wait_recv()
    arr2[...] = arr[...].astype(F32).reshape(arr2.shape).astype(BF)

    @pl.loop(0, medges // TILE)
    def _(t):
        rows = pl.ds(pl.multiple_of(t * TILE, TILE), TILE)
        first = acc2[rows, :] + dot(g_msnd[rows, :], arr2[...])
        second = dot(silu(first).astype(BF), v_pw[3]) + v_bias[3, 1:2, :]
        msg[rows, :] = norm(second, v_gain[3:4, :]).astype(BF)

    scatters = []
    for c in range(NC):
        sums = dot(r_rcv[...], msg[:, cols[c]]).astype(BF)
        part2[c] = sums.reshape(n_band, share, wc)
        scatters.append(scatter_start(c, part2, far2, near2, rt_s, rt_r))
    relays = []
    for c in range(NC):
        relays.append(scatter_relay(c, scatters[c][0], part2, far2, relay2, relayed2, rt_s, rt_r))
        sent += [*scatters[c], relays[c]]
    first = base_fin[...]
    for c in range(NC):
        scatters[c][1].wait_recv()
        relays[c].wait_recv()
        total = part2[c, band].astype(F32) + near2[c].astype(F32) + relayed2[c].astype(F32)
        first = first + dot(total.astype(BF), v_fw[1, cols[c], :])
    tail = norm(dot(silu(first).astype(BF), v_fw[2]) + v_bias[4, 1:2, :], v_gain[4:5, :])
    for c in range(NC):
        v_mo[:, cols[c]] = (mid[c, band].astype(F32) + tail[:, cols[c]]).astype(BF)
    mesh_copy = pltpu.make_async_copy(v_mo, mesh_out, out_sem.at[1])
    mesh_copy.start()
    for copy in sent:
        copy.wait_send()
    everyone.wait_send()
    grid_copy.wait()
    mesh_copy.wait()


def per_device(n_blk, n_band, *args):
    (grid_nodes, enc_edges, enc_sender, enc_slot, enc_slot_node, mesh_nodes, mesh_edges,
     mesh_sender, mesh_receiver, mesh_send_node, *params) = args

    def folded(index):
        return index.reshape(-1, LANES)

    args = (grid_nodes, enc_edges, folded(enc_sender), folded(enc_slot), enc_slot_node, mesh_nodes,
            mesh_edges, folded(mesh_sender), folded(mesh_receiver), mesh_send_node, *params)
    width = mesh_nodes.shape[1]
    wc = width // NC
    nodes = mesh_nodes.shape[0]
    share = nodes // n_band
    grid_rows = grid_nodes.shape[0]
    edges, medges = enc_edges.shape[0], mesh_edges.shape[0]
    slots = NEIGH * CAP
    requests = mesh_send_node.shape[1]
    vm = pltpu.VMEM
    dma = pltpu.SemaphoreType.DMA
    scratch = [vm(a.shape, a.dtype) for a in args]
    scratch += [vm((grid_rows, width), BF), vm((share, width), BF)]
    window = (NC, NEIGH, CAP, wc)
    shares, piece = (NC, n_band, share, wc), (NC, share, wc)
    boxes = (n_blk, requests // n_blk, width)
    scratch += [vm(window, BF)] * 4
    scratch += [vm(shares, BF)] + [vm(piece, BF)] * 4
    scratch += [vm(shares, BF), vm(boxes, BF), vm(boxes, BF), vm((requests, width), BF)]
    scratch += [vm(shares, BF)] + [vm(piece, BF)] * 4
    scratch += [
        vm((slots, nodes), BF), vm((edges, slots), BF), vm((slots, edges), BF),
        vm((edges, grid_rows), BF), vm((n_band, share, slots), BF), vm((requests, nodes), BF),
        vm((medges, requests), BF), vm((8, LANES), BF), vm((nodes, medges), BF),
    ]
    scratch += [
        vm((grid_rows, width), BF), vm((edges, width), F32), vm((medges, width), F32),
        vm((edges, width), F32), vm((max(edges, medges), width), BF), vm((share, width), F32),
        vm((share, width), F32), vm((slots, width), BF), vm((nodes, width), BF),
    ]
    near = len(WINDOWS)
    scratch += [dma((24,)), dma((2,))]
    scratch += [dma((NC, near))] * 4
    scratch += [dma((NC, 3))] * 4
    scratch += [dma, dma] + [dma((NC, 3))] * 2
    anywhere = pl.BlockSpec(memory_space=pl.ANY)
    return pl.pallas_call(
        kernel,
        out_shape=(
            jax.ShapeDtypeStruct((grid_rows, width), BF),
            jax.ShapeDtypeStruct((share, width), BF),
        ),
        in_specs=[anywhere] * len(args),
        out_specs=(anywhere, anywhere),
        scratch_shapes=scratch,
        compiler_params=pltpu.CompilerParams(
            collective_id=0, has_side_effects=True, vmem_limit_bytes=56 * 1024 * 1024
        ),
        name="encoder_processor",
    )(*args)


def solution(mesh):
    rows = P(("blk", "band"), None)
    flat = P(("blk", "band"))
    in_specs = (rows, rows, flat, flat, rows, P("blk", None), rows, flat, flat, rows) + (P(),) * 7
    n_blk, n_band = mesh.shape["blk"], mesh.shape["band"]

    def step(*args):
        return per_device(n_blk, n_band, *args)

    return jax.shard_map(
        step, mesh=mesh, in_specs=in_specs, out_specs=(rows, rows), check_vma=False
    )
```

time: 175 us -> 83.3 us (0.48)
  Pallas kernels: 0 us -> 77.8 us
  waiting for transfers between devices: 51 us -> 0 us
  starting transfers between devices: 43.7 us -> 0 us
  matrix products: 30.6 us -> 0 us
  local copies, waits for them, and re-layouts: 30.3 us -> 3.46 us
  other arithmetic: 16.7 us -> 0 us
    pallas_call x0 -> x1, Pallas kernels: none -> 77.8 us  [per_device(): pl.pallas_call(kernel, out_shape=(jax.ShapeDtypeStruct((grid_rows, width)...]
    all_to_all x3 -> x0, waiting for transfers between devices: 39.1 us -> none  [the longest x1 23 us: from_everyone(): return lax.all_to_all(copies, axis, split_axis=0, concat_axis=0, tiled=True)]
    dot_general x13 -> x0, matrix products: 30.6 us -> none  [the longest x5 16.4 us: dense_tail(): jnp.dot(hidden, second_weight, preferred_element_type=jnp.float32)]
    ppermute x14 -> x0, starting transfers between devices: 25.7 us -> none  [shifted(): return lax.ppermute(block, axis, route)]
    gather x6 -> x0, local copies, waits for them, and re-layouts: 25.2 us -> none  [the longest x1 5.06 us: per_device(): jnp.take(target_keys, mesh_receiver, axis=0).astype(jnp.float32)]
    all_to_all x3 -> x0, starting transfers between devices: 18 us -> none  [the longest x1 9.86 us: per_device(): lax.all_to_all(sender_rows, 'blk', split_axis=0, concat_axis=0, tiled=True)]
    ppermute x14 -> x0, waiting for transfers between devices: 11.9 us -> none  [shifted(): return lax.ppermute(block, axis, route)]
    reduce_sum x7 -> x0, other arithmetic: 7.12 us -> none  [the longest x5 4.51 us: layer_norm(): spread = jnp.mean(center * center, axis=-1, keepdims=True)]
  transfers between devices with their start and end apart: 17 -> 0, of which waited for: 9 -> 0; matrix products, arithmetic and copies ran while one was open for 14% -> 0% of each run, Pallas kernels for 0% -> 0%
where the time goes in v1:
time: 83.3 us; the launch traced here: 81.9 us
  Pallas kernels  77.8 us (93%)
  local copies, waits for them, and re-layouts  3.46 us (4%)
    pallas_call x1, Pallas kernels, per_device(): pl.pallas_call(kernel, out_shape=(jax.ShapeDtypeStruct((grid_rows, width)...  77.8 us
    unnamed x2, local copies, waits for them, and re-layouts  3.46 us

profile of v1, /device:TPU:32, one launch (start us, length us, event | category | flops | bytes accessed | tf_op | source)
XLA Modules:
  0.0 81.9 jit_solution(11666641947661086445)
XLA Ops:
  0.6 77.8 %encoder_processor.1 = (bf16[512,512]{1,0:T(8,128)(2,1)}, bf16[160,512]{1,0:T(8,128)(2,1)}) custom-call(bf16[512,512]{1,0:T(8,128)(2,1)} %grid_nodes.1, bf16[1024,512]{1,0:T(8,128)(2,1)} %enc_edges.1, s32[8,128]{1,0:T(8,128)} %bitcast.4, s32[8,128]{1,0:T(8,128)} %bitcast.5, s32[1,512]{1,0:T(1,128)} %enc_slot_node.1, bf16[640,512]{1,0:T(8,128)(2,1)} %mesh_nodes.1, ...), custom_call_target="tpu_custom_call" | custom-call | tf_op jit(solution)/shard_map/encoder_processor/pallas_call | solution.py:428
  78.4 1.9 %copy.21 = bf16[512,512]{1,0:T(8,128)(2,1)} copy(bf16[512,512]{1,0:T(8,128)(2,1)} %get-tuple-element.4) | data formatting | bytes 1048576
  80.3 1.6 %copy.22 = bf16[160,512]{1,0:T(8,128)(2,1)} copy(bf16[160,512]{1,0:T(8,128)(2,1)} %get-tuple-element.5) | data formatting | bytes 327680

commit v2 on v1

--- a/solution.py
+++ b/solution.py
@@ -10,6 +10,7 @@
 MIDDLE = NEIGH // 2
 WINDOWS = [k for k in range(NEIGH) if k != MIDDLE]
 NC = 2
+NS = 4
 MESH = pl.DeviceIdType.MESH
 BF = jnp.bfloat16
 F32 = jnp.float32
@@ -57,7 +58,7 @@
     grid_out, mesh_out,
     v_grid, v_ee, v_esnd, v_eslot, v_esn, v_mesh, v_me, v_msnd, v_mrcv, v_msn,
     v_gw, v_ew, v_nw, v_pw, v_fw, v_bias, v_gain, v_go, v_mo,
-    keys, arrived, ssum, landed, part, far, near, relay, relayed, mid, srows, arr, arr2,
+    keys, arrived, ssum, landed, part, came, mid, srows, arr, arr2,
     part2, far2, near2, relay2, relayed2,
     g_key, g_slot, s_slot, g_snd, p_node, g_send, g_msnd, g_rcv, r_rcv,
     sproj, acc, acc2, opart, msg, base_mid, base_fin, gsel, tkeys,
@@ -72,6 +73,7 @@
     across = lax.rem(band + 2, n_band)
     width = v_mesh.shape[1]
     wc = width // NC
+    ws = width // NS
     nodes = v_mesh.shape[0]
     share = nodes // n_band
     slots = NEIGH * CAP
@@ -102,7 +104,7 @@
             barrier, inc=1, device_id=(lax.rem(blk + r, n_blk), band), device_id_type=MESH
         )
 
-    for peer in (left, right):
+    for peer in (left, right, across):
         pl.semaphore_signal(barrier, inc=1, device_id=(blk, peer), device_id_type=MESH)
 
     load("grid", grid_nodes, v_grid)
@@ -144,7 +146,7 @@
         projected = dot(gsel[...], v_ew[2, :, cols[c]]).astype(BF)
         keys[c] = projected.reshape(NEIGH, CAP, wc)
         if c == 0:
-            pl.semaphore_wait(barrier, n_blk - 1 + 2)
+            pl.semaphore_wait(barrier, n_blk - 1 + n_band - 1)
         copies = []
         for i, k in enumerate(WINDOWS):
             copy = remote(
@@ -161,7 +163,7 @@
     sproj[...] = dot(v_grid[...], v_ew[1]).astype(BF)
     ready("esnd", "eslot")
 
-    @pl.loop(0, edges // LANES)
+    @pl.loop(0, edges // LANES, unroll=2)
     def _(r):
         rows = pl.ds(pl.multiple_of(r * LANES, LANES), LANES)
         g_snd[rows, :] = rows_select(down_column(v_esnd[pl.ds(r, 1), :]), v_grid.shape[0])
@@ -172,7 +174,7 @@
     ready("bias", "gain", "ee", "ew0")
     TILE = 256
 
-    @pl.loop(0, edges // TILE)
+    @pl.loop(0, edges // TILE, unroll=True)
     def _(t):
         rows = pl.ds(pl.multiple_of(t * TILE, TILE), TILE)
         acc[rows, :] = (
@@ -185,7 +187,7 @@
         for copy in key_copies[c]:
             copy.wait_recv()
 
-        @pl.loop(0, edges // TILE)
+        @pl.loop(0, edges // TILE, unroll=True)
         def _(t):
             rows = pl.ds(pl.multiple_of(t * TILE, TILE), TILE)
             first = acc[rows, cols[c]] + dot(g_slot[rows, :], arrived[c].reshape(slots, wc))
@@ -198,23 +200,26 @@
                 msg[rows, :] = norm(second + v_bias[1, 1:2, :], v_gain[1:2, :]).astype(BF)
 
     sum_copies = []
-    for c in range(NC):
-        ssum[c] = dot(s_slot[...], msg[:, cols[c]]).astype(BF).reshape(NEIGH, CAP, wc)
-        copies = []
-        for i, k in enumerate(WINDOWS):
-            copy = remote(
-                ssum.at[c, k], landed.at[c, k], cs_s.at[c, i], cs_r.at[c, i],
-                lax.rem(blk + k - MIDDLE + n_blk, n_blk), band,
-            )
-            copy.start()
-            copies.append(copy)
-        sum_copies.append(copies)
-        sent += copies
-        landed[c, MIDDLE] = ssum[c, MIDDLE]
+    for h in range(NC):
+        halves = dot(s_slot[...], msg[:, cols[h]]).astype(BF)
+        for c in range(h * NS // NC, (h + 1) * NS // NC):
+            low = c * ws - h * wc
+            ssum[c] = halves[:, low : low + ws].reshape(NEIGH, CAP, ws)
+            copies = []
+            for i, k in enumerate(WINDOWS):
+                copy = remote(
+                    ssum.at[c, k], landed.at[c, k], cs_s.at[c, i], cs_r.at[c, i],
+                    lax.rem(blk + k - MIDDLE + n_blk, n_blk), band,
+                )
+                copy.start()
+                copies.append(copy)
+            sum_copies.append(copies)
+            sent += copies
+            landed[c, MIDDLE] = ssum[c, MIDDLE]
 
     for r in range(slots // LANES):
         select = cols_select(v_esn[0:1, r * LANES : (r + 1) * LANES], nodes)
-        p_node[:, :, r * LANES : (r + 1) * LANES] = select.reshape(n_band, share, LANES)
+        p_node[:, r * LANES : (r + 1) * LANES] = select
     ready("nw0", "nw1", "nw2", "msn", "msnd", "mrcv")
     own_rows = pl.ds(pl.multiple_of(band * share, 32), share)
     base_mid[...] = dot(v_mesh[own_rows, :], v_nw[0]) + v_bias[2, 0:1, :]
@@ -241,25 +246,27 @@
         copy.start()
         return copy
 
-    scatters = []
-    for c in range(NC):
+    pieces = []
+    for c in range(NS):
         for copy in sum_copies[c]:
             copy.wait_recv()
-        sums = landed[c].reshape(slots, wc)
-        for s in range(n_band):
-            part[c, s] = dot(p_node[s], sums).astype(BF)
-        scatters.append(scatter_start(c, part, far, near, rs_s, rs_r))
-    relays = []
-    for c in range(NC):
-        relays.append(scatter_relay(c, scatters[c][0], part, far, relay, relayed, rs_s, rs_r))
-        sent += [*scatters[c], relays[c]]
+        sums = dot(p_node[...], landed[c].reshape(slots, ws)).astype(BF)
+        part[c] = sums.reshape(n_band, share, ws)
+        copies = []
+        for i, peer in enumerate((right, left, across)):
+            copy = remote(part.at[c, peer], came.at[c, i], rs_s.at[c, i], rs_r.at[c, i], blk, peer)
+            copy.start()
+            copies.append(copy)
+        pieces.append(copies)
+        sent += copies
 
     first = base_mid[...]
-    for c in range(NC):
-        scatters[c][1].wait_recv()
-        relays[c].wait_recv()
-        total = part[c, band].astype(F32) + near[c].astype(F32) + relayed[c].astype(F32)
-        first = first + dot(total.astype(BF), v_nw[1, cols[c], :])
+    for c in range(NS):
+        total = part[c, band].astype(F32)
+        for i, copy in enumerate(pieces[c]):
+            copy.wait_recv()
+            total = total + came[c, i].astype(F32)
+        first = first + dot(total.astype(BF), v_nw[1, c * ws : (c + 1) * ws, :])
     tail = norm(dot(silu(first).astype(BF), v_nw[2]) + v_bias[2, 1:2, :], v_gain[2:3, :])
     own_mid = (v_mesh[own_rows, :].astype(F32) + tail).astype(BF)
     for c in range(NC):
@@ -276,14 +283,6 @@
         for c in range(NC):
             gathers[c, hop].start()
 
-    ready("me", "pw")
-
-    @pl.loop(0, medges // LANES)
-    def _(r):
-        rows = pl.ds(pl.multiple_of(r * LANES, LANES), LANES)
-        acc2[rows, :] = dot(v_me[rows, :], v_pw[0]) + v_bias[3, 0:1, :]
-        g_msnd[rows, :] = rows_select(down_column(v_msnd[pl.ds(r, 1), :]), slots)
-
     for c in range(NC):
         first_peer, other_peer = toward(c)
         gathers[c, 0].wait_recv()
@@ -291,7 +290,15 @@
             mid.at[c, other_peer], mid.at[c, other_peer], ag_s.at[c, 2], ag_r.at[c, 2], blk, first_peer
         )
         gathers[c, 2].start()
-    base_fin[...] = v_bias[4, 0:1, :] + jnp.zeros_like(base_fin)
+
+    ready("me", "pw")
+
+    @pl.loop(0, medges // LANES, unroll=2)
+    def _(r):
+        rows = pl.ds(pl.multiple_of(r * LANES, LANES), LANES)
+        acc2[rows, :] = dot(v_me[rows, :], v_pw[0]) + v_bias[3, 0:1, :]
+        g_msnd[rows, :] = rows_select(down_column(v_msnd[pl.ds(r, 1), :]), slots)
+
     requested = None
     for c in range(NC):
         gathers[c, 1].wait_recv()
@@ -317,7 +324,7 @@
         tk = term if tk is None else tk + term
     tkeys[...] = tk.astype(BF)
 
-    @pl.loop(0, medges // LANES)
+    @pl.loop(0, medges // LANES, unroll=2)
     def _(r):
         rows = pl.ds(pl.multiple_of(r * LANES, LANES), LANES)
         receiver_row = v_mrcv[pl.ds(r, 1), :]
@@ -327,7 +334,7 @@
 
     ready("gw")
 
-    @pl.loop(0, v_grid.shape[0] // TILE)
+    @pl.loop(0, v_grid.shape[0] // TILE, unroll=True)
     def _(t):
         rows = pl.ds(pl.multiple_of(t * TILE, TILE), TILE)
         first = dot(v_grid[rows, :], v_gw[0]) + v_bias[0, 0:1, :]
@@ -347,7 +354,7 @@
     everyone.wait_recv()
     arr2[...] = arr[...].astype(F32).reshape(arr2.shape).astype(BF)
 
-    @pl.loop(0, medges // TILE)
+    @pl.loop(0, medges // TILE, unroll=True)
     def _(t):
         rows = pl.ds(pl.multiple_of(t * TILE, TILE), TILE)
         first = acc2[rows, :] + dot(g_msnd[rows, :], arr2[...])
@@ -379,6 +386,24 @@
     everyone.wait_send()
     grid_copy.wait()
     mesh_copy.wait()
+
+
+def handed_on(grid_in, mesh_in, grid_out, mesh_out, v_mesh, v_grid, sem):
+    pieces = v_grid.shape[0]
+    rows = v_grid.shape[1]
+    copies = [(mesh_in, v_mesh, mesh_out)]
+    for i in range(pieces):
+        part = pl.ds(i * rows, rows)
+        copies.append((grid_in.at[part], v_grid.at[i], grid_out.at[part]))
+    come = [pltpu.make_async_copy(a, v, sem.at[0, i]) for i, (a, v, _) in enumerate(copies)]
+    leave = [pltpu.make_async_copy(v, b, sem.at[1, i]) for i, (_, v, b) in enumerate(copies)]
+    for copy in come:
+        copy.start()
+    for first, second in zip(come, leave):
+        first.wait()
+        second.start()
+    for copy in leave:
+        copy.wait()
 
 
 def per_device(n_blk, n_band, *args):
@@ -405,13 +430,14 @@
     window = (NC, NEIGH, CAP, wc)
     shares, piece = (NC, n_band, share, wc), (NC, share, wc)
     boxes = (n_blk, requests // n_blk, width)
-    scratch += [vm(window, BF)] * 4
-    scratch += [vm(shares, BF)] + [vm(piece, BF)] * 4
+    ws = width // NS
+    scratch += [vm(window, BF)] * 2 + [vm((NS, NEIGH, CAP, ws), BF)] * 2
+    scratch += [vm((NS, n_band, share, ws), BF), vm((NS, n_band - 1, share, ws), BF)]
     scratch += [vm(shares, BF), vm(boxes, BF), vm(boxes, BF), vm((requests, width), BF)]
     scratch += [vm(shares, BF)] + [vm(piece, BF)] * 4
     scratch += [
         vm((slots, nodes), BF), vm((edges, slots), BF), vm((slots, edges), BF),
-        vm((edges, grid_rows), BF), vm((n_band, share, slots), BF), vm((requests, nodes), BF),
+        vm((edges, grid_rows), BF), vm((nodes, slots), BF), vm((requests, nodes), BF),
         vm((medges, requests), BF), vm((8, LANES), BF), vm((nodes, medges), BF),
     ]
     scratch += [
@@ -421,11 +447,11 @@
     ]
     near = len(WINDOWS)
     scratch += [dma((24,)), dma((2,))]
-    scratch += [dma((NC, near))] * 4
-    scratch += [dma((NC, 3))] * 4
+    scratch += [dma((NC, near))] * 2 + [dma((NS, near))] * 2
+    scratch += [dma((NS, 3))] * 2 + [dma((NC, 3))] * 2
     scratch += [dma, dma] + [dma((NC, 3))] * 2
     anywhere = pl.BlockSpec(memory_space=pl.ANY)
-    return pl.pallas_call(
+    results = pl.pallas_call(
         kernel,
         out_shape=(
             jax.ShapeDtypeStruct((grid_rows, width), BF),
@@ -439,6 +465,14 @@
         ),
         name="encoder_processor",
     )(*args)
+    return pl.pallas_call(
+        handed_on,
+        out_shape=tuple(jax.ShapeDtypeStruct(r.shape, r.dtype) for r in results),
+        in_specs=[anywhere] * 2,
+        out_specs=(anywhere, anywhere),
+        scratch_shapes=[vm((share, width), BF), vm((4, grid_rows // 4, width), BF), dma((2, 5))],
+        name="handed_on",
+    )(*results)
 
 
 def solution(mesh):

time: 83.3 us -> 78.1 us (0.938)
  local copies, waits for them, and re-layouts: 3.46 us -> 0 us
  Pallas kernels: 77.8 us -> 76.2 us
    pallas_call x1, Pallas kernels: 77.8 us -> 74.3 us  [per_device(): pl.pallas_call(kernel, out_shape=(jax.ShapeDtypeStruct((grid_rows, width)...]
    unnamed x2 -> x0, local copies, waits for them, and re-layouts: 3.46 us -> none
    pallas_call x0 -> x1, Pallas kernels: none -> 1.92 us  [per_device(): pl.pallas_call(handed_on, out_shape=tuple((jax.ShapeDtypeStruct(r.shape,...]
where the time goes in v2:
time: 78.1 us; the launch traced here: 77 us
  Pallas kernels  76.2 us (98%)
  between operations  0.81 us (1%)
    pallas_call x1, Pallas kernels, per_device(): pl.pallas_call(kernel, out_shape=(jax.ShapeDtypeStruct((grid_rows, width)...  74.3 us
    pallas_call x1, Pallas kernels, per_device(): pl.pallas_call(handed_on, out_shape=tuple((jax.ShapeDtypeStruct(r.shape,...  1.92 us

profile of v2, /device:TPU:32, one launch (start us, length us, event | category | flops | bytes accessed | tf_op | source)
XLA Modules:
  0.0 77.0 jit_solution(4891952520043315442)
XLA Ops:
  0.6 74.3 %encoder_processor.1 = (bf16[512,512]{1,0:T(8,128)(2,1)}, bf16[160,512]{1,0:T(8,128)(2,1)}) custom-call(bf16[512,512]{1,0:T(8,128)(2,1)} %grid_nodes.1, bf16[1024,512]{1,0:T(8,128)(2,1)} %enc_edges.1, s32[8,128]{1,0:T(8,128)} %bitcast.4, s32[8,128]{1,0:T(8,128)} %bitcast.5, s32[1,512]{1,0:T(1,128)} %enc_slot_node.1, bf16[640,512]{1,0:T(8,128)(2,1)} %mesh_nodes.1, ...), custom_call_target="tpu_custom_call" | custom-call | tf_op jit(solution)/shard_map/encoder_processor/pallas_call | solution.py:454
  75.0 1.9 %handed_on.1 = (bf16[512,512]{1,0:T(8,128)(2,1)}, bf16[160,512]{1,0:T(8,128)(2,1)}) custom-call(bf16[512,512]{1,0:T(8,128)(2,1)} %get-tuple-element.4.grid_in, bf16[160,512]{1,0:T(8,128)(2,1)} %get-tuple-element.5.mesh_in), custom_call_target="tpu_custom_call" | custom-call | tf_op jit(solution)/shard_map/handed_on/pallas_call | solution.py:468

commit v3 on v2

--- a/solution.py
+++ b/solution.py
@@ -11,6 +11,7 @@
 WINDOWS = [k for k in range(NEIGH) if k != MIDDLE]
 NC = 2
 NS = 4
+NM = 4
 MESH = pl.DeviceIdType.MESH
 BF = jnp.bfloat16
 F32 = jnp.float32
@@ -74,6 +75,7 @@
     width = v_mesh.shape[1]
     wc = width // NC
     ws = width // NS
+    wm = width // NM
     nodes = v_mesh.shape[0]
     share = nodes // n_band
     slots = NEIGH * CAP
@@ -220,12 +222,27 @@
     for r in range(slots // LANES):
         select = cols_select(v_esn[0:1, r * LANES : (r + 1) * LANES], nodes)
         p_node[:, r * LANES : (r + 1) * LANES] = select
-    ready("nw0", "nw1", "nw2", "msn", "msnd", "mrcv")
+    ready("nw0", "nw1", "nw2", "msn", "msnd", "mrcv", "me", "pw")
     own_rows = pl.ds(pl.multiple_of(band * share, 32), share)
-    base_mid[...] = dot(v_mesh[own_rows, :], v_nw[0]) + v_bias[2, 0:1, :]
-    for r in range(v_msn.shape[1] // LANES):
-        column = down_column(v_msn[0:1, r * LANES : (r + 1) * LANES])
-        g_send[r * LANES : (r + 1) * LANES, :] = rows_select(column, nodes)
+
+    def fill_base():
+        base_mid[...] = dot(v_mesh[own_rows, :], v_nw[0]) + v_bias[2, 0:1, :]
+
+    def fill_send():
+        for r in range(v_msn.shape[1] // LANES):
+            column = down_column(v_msn[0:1, r * LANES : (r + 1) * LANES])
+            g_send[r * LANES : (r + 1) * LANES, :] = rows_select(column, nodes)
+
+    def fill_edges(part, parts):
+        count = medges // LANES // parts
+
+        @pl.loop(part * count, (part + 1) * count, unroll=2)
+        def _(r):
+            rows = pl.ds(pl.multiple_of(r * LANES, LANES), LANES)
+            acc2[rows, :] = dot(v_me[rows, :], v_pw[0]) + v_bias[3, 0:1, :]
+            g_msnd[rows, :] = rows_select(down_column(v_msnd[pl.ds(r, 1), :]), slots)
+
+    fills = [fill_base, fill_send, lambda: fill_edges(0, 2), lambda: fill_edges(1, 2)]
 
     def toward(c):
         return (left, right) if c == 0 else (right, left)
@@ -259,6 +276,8 @@
             copies.append(copy)
         pieces.append(copies)
         sent += copies
+        if c < NS - 1:
+            fills[c]()
 
     first = base_mid[...]
     for c in range(NS):
@@ -269,60 +288,59 @@
         first = first + dot(total.astype(BF), v_nw[1, c * ws : (c + 1) * ws, :])
     tail = norm(dot(silu(first).astype(BF), v_nw[2]) + v_bias[2, 1:2, :], v_gain[2:3, :])
     own_mid = (v_mesh[own_rows, :].astype(F32) + tail).astype(BF)
-    for c in range(NC):
-        mid[c, band] = own_mid[:, cols[c]]
+    mid[band] = own_mid
 
     gathers = {}
-    for c in range(NC):
-        first_peer, other_peer = toward(c)
-        for hop, peer in ((0, first_peer), (1, other_peer)):
-            gathers[c, hop] = remote(
-                mid.at[c, band], mid.at[c, band], ag_s.at[c, hop], ag_r.at[c, hop], blk, peer
-            )
-    for hop in range(2):
-        for c in range(NC):
-            gathers[c, hop].start()
-
-    for c in range(NC):
-        first_peer, other_peer = toward(c)
-        gathers[c, 0].wait_recv()
-        gathers[c, 2] = remote(
-            mid.at[c, other_peer], mid.at[c, other_peer], ag_s.at[c, 2], ag_r.at[c, 2], blk, first_peer
+
+    def spread(m, hop):
+        first_peer, other_peer = toward(m % 2)
+        owner = other_peer if hop == 2 else band
+        block = mid.at[owner, :, m * wm : (m + 1) * wm]
+        gathers[m, hop] = remote(
+            block, block, ag_s.at[m, hop], ag_r.at[m, hop], blk, other_peer if hop == 1 else first_peer
         )
-        gathers[c, 2].start()
-
-    ready("me", "pw")
-
-    @pl.loop(0, medges // LANES, unroll=2)
-    def _(r):
-        rows = pl.ds(pl.multiple_of(r * LANES, LANES), LANES)
-        acc2[rows, :] = dot(v_me[rows, :], v_pw[0]) + v_bias[3, 0:1, :]
-        g_msnd[rows, :] = rows_select(down_column(v_msnd[pl.ds(r, 1), :]), slots)
-
-    requested = None
-    for c in range(NC):
-        gathers[c, 1].wait_recv()
-        gathers[c, 2].wait_recv()
-        picked = dot(g_send[...], mid[c].reshape(nodes, wc)).astype(BF)
-        term = dot(picked, v_pw[1, cols[c], :])
-        requested = term if requested is None else requested + term
+        gathers[m, hop].start()
+
+    def spread_own(half):
+        for hop in range(2):
+            for m in half:
+                spread(m, hop)
+
+    def spread_on(half):
+        for m in half:
+            gathers[m, 0].wait_recv()
+            spread(m, 2)
+
+    def pick(h, half):
+        for m in half:
+            gathers[m, 1].wait_recv()
+            gathers[m, 2].wait_recv()
+        picked = dot(g_send[...], mid[:, :, cols[h]].reshape(nodes, wc))
+        srows[h] = picked.reshape(srows.shape[1:]).astype(BF)
+
+    def to_everyone(h):
+        @pl.loop(0, n_blk - 1)
+        def _(i):
+            step = (i + 1) // 2
+            r = n_blk // 2 + step * (1 - 2 * lax.rem(i, 2))
+            to = lax.rem(blk + r, n_blk)
+            remote(srows.at[h, to], arr.at[h, blk], aa_s.at[h], aa_r.at[h], to, band).start()
+
+        arr[h, blk] = srows[h, blk]
+
+    halves = [range(h * NM // NC, (h + 1) * NM // NC) for h in range(NC)]
+    spread_own(halves[0])
+    spread_on(halves[0])
+    spread_own(halves[1])
+    pick(0, halves[0])
+    spread_on(halves[1])
+    to_everyone(0)
+    pick(1, halves[1])
+    to_everyone(1)
+    fills[NS - 1]()
     sent += list(gathers.values())
-    srows[...] = requested.reshape(srows.shape).astype(BF)
-
-    @pl.loop(0, n_blk - 1)
-    def _(i):
-        step = (i + 1) // 2
-        r = n_blk // 2 + step * (1 - 2 * lax.rem(i, 2))
-        to = lax.rem(blk + r, n_blk)
-        remote(srows.at[to], arr.at[blk], aa_s, aa_r, to, band).start()
-
-    arr[blk] = srows[blk]
-
-    tk = None
-    for c in range(NC):
-        term = dot(mid[c].reshape(nodes, wc), v_pw[2, cols[c], :])
-        tk = term if tk is None else tk + term
-    tkeys[...] = tk.astype(BF)
+
+    tkeys[...] = dot(mid[...].reshape(nodes, width), v_pw[2]).astype(BF)
 
     @pl.loop(0, medges // LANES, unroll=2)
     def _(r):
@@ -344,15 +362,23 @@
     grid_copy = pltpu.make_async_copy(v_go, grid_out, out_sem.at[0])
     grid_copy.start()
     ready("fw")
-    fin = v_bias[4, 0:1, :]
-    for c in range(NC):
-        fin = fin + dot(mid[c, band], v_fw[0, cols[c], :])
-    base_fin[...] = fin
+    base_fin[...] = dot(mid[band], v_fw[0]) + v_bias[4, 0:1, :]
 
     blocks = pl.ds(0, n_blk - 1)
-    everyone = remote(srows.at[blocks], arr.at[blocks], aa_s, aa_r, blk, band)
-    everyone.wait_recv()
-    arr2[...] = arr[...].astype(F32).reshape(arr2.shape).astype(BF)
+    everyone = [
+        remote(srows.at[h, blocks], arr.at[h, blocks], aa_s.at[h], aa_r.at[h], blk, band)
+        for h in range(NC)
+    ]
+    requested = None
+    for h in range(NC):
+        everyone[h].wait_recv()
+        raw = arr[h].astype(F32).reshape(arr2.shape[0], wc).astype(BF)
+        term = dot(raw, v_pw[1, cols[h], :])
+        if h < NC - 1:
+            opart[0 : arr2.shape[0], :] = term if requested is None else opart[0 : arr2.shape[0], :] + term
+            requested = opart
+        else:
+            arr2[...] = (opart[0 : arr2.shape[0], :] + term).astype(BF)
 
     @pl.loop(0, medges // TILE, unroll=True)
     def _(t):
@@ -378,12 +404,13 @@
         first = first + dot(total.astype(BF), v_fw[1, cols[c], :])
     tail = norm(dot(silu(first).astype(BF), v_fw[2]) + v_bias[4, 1:2, :], v_gain[4:5, :])
     for c in range(NC):
-        v_mo[:, cols[c]] = (mid[c, band].astype(F32) + tail[:, cols[c]]).astype(BF)
+        v_mo[:, cols[c]] = (mid[band, :, cols[c]].astype(F32) + tail[:, cols[c]]).astype(BF)
     mesh_copy = pltpu.make_async_copy(v_mo, mesh_out, out_sem.at[1])
     mesh_copy.start()
     for copy in sent:
         copy.wait_send()
-    everyone.wait_send()
+    for copy in everyone:
+        copy.wait_send()
     grid_copy.wait()
     mesh_copy.wait()
 
@@ -429,11 +456,11 @@
     scratch += [vm((grid_rows, width), BF), vm((share, width), BF)]
     window = (NC, NEIGH, CAP, wc)
     shares, piece = (NC, n_band, share, wc), (NC, share, wc)
-    boxes = (n_blk, requests // n_blk, width)
+    boxes = (NC, n_blk, requests // n_blk, wc)
     ws = width // NS
     scratch += [vm(window, BF)] * 2 + [vm((NS, NEIGH, CAP, ws), BF)] * 2
     scratch += [vm((NS, n_band, share, ws), BF), vm((NS, n_band - 1, share, ws), BF)]
-    scratch += [vm(shares, BF), vm(boxes, BF), vm(boxes, BF), vm((requests, width), BF)]
+    scratch += [vm((n_band, share, width), BF), vm(boxes, BF), vm(boxes, BF), vm((requests, width), BF)]
     scratch += [vm(shares, BF)] + [vm(piece, BF)] * 4
     scratch += [
         vm((slots, nodes), BF), vm((edges, slots), BF), vm((slots, edges), BF),
@@ -448,8 +475,8 @@
     near = len(WINDOWS)
     scratch += [dma((24,)), dma((2,))]
     scratch += [dma((NC, near))] * 2 + [dma((NS, near))] * 2
-    scratch += [dma((NS, 3))] * 2 + [dma((NC, 3))] * 2
-    scratch += [dma, dma] + [dma((NC, 3))] * 2
+    scratch += [dma((NS, 3))] * 2 + [dma((NM, 3))] * 2
+    scratch += [dma((NC,))] * 2 + [dma((NC, 3))] * 2
     anywhere = pl.BlockSpec(memory_space=pl.ANY)
     results = pl.pallas_call(
         kernel,

time: 78.1 us -> 76.5 us (0.980); the launches traced: 77 us -> 76.4 us
  no operation moved by 1% of the time
where the time goes in v3:
time: 76.5 us; the launch traced here: 76.4 us
  Pallas kernels  75.6 us (99%)
  between operations  0.81 us (1%)
    pallas_call x1, Pallas kernels, per_device(): pl.pallas_call(kernel, out_shape=(jax.ShapeDtypeStruct((grid_rows, width)...  73.7 us
    pallas_call x1, Pallas kernels, per_device(): pl.pallas_call(handed_on, out_shape=tuple((jax.ShapeDtypeStruct(r.shape,...  1.92 us

profile of v3, /device:TPU:32, one launch (start us, length us, event | category | flops | bytes accessed | tf_op | source)
XLA Modules:
  0.0 76.4 jit_solution(9347878541365438240)
XLA Ops:
  0.6 73.7 %encoder_processor.1 = (bf16[512,512]{1,0:T(8,128)(2,1)}, bf16[160,512]{1,0:T(8,128)(2,1)}) custom-call(bf16[512,512]{1,0:T(8,128)(2,1)} %grid_nodes.1, bf16[1024,512]{1,0:T(8,128)(2,1)} %enc_edges.1, s32[8,128]{1,0:T(8,128)} %bitcast.4, s32[8,128]{1,0:T(8,128)} %bitcast.5, s32[1,512]{1,0:T(1,128)} %enc_slot_node.1, bf16[640,512]{1,0:T(8,128)(2,1)} %mesh_nodes.1, ...), custom_call_target="tpu_custom_call" | custom-call | tf_op jit(solution)/shard_map/encoder_processor/pallas_call | solution.py:481
  74.3 1.9 %handed_on.1 = (bf16[512,512]{1,0:T(8,128)(2,1)}, bf16[160,512]{1,0:T(8,128)(2,1)}) custom-call(bf16[512,512]{1,0:T(8,128)(2,1)} %get-tuple-element.4.grid_in, bf16[160,512]{1,0:T(8,128)(2,1)} %get-tuple-element.5.mesh_in), custom_call_target="tpu_custom_call" | custom-call | tf_op jit(solution)/shard_map/handed_on/pallas_call | solution.py:495

commit v4 on v3

--- a/solution.py
+++ b/solution.py
@@ -56,14 +56,14 @@
     grid_nodes, enc_edges, enc_sender, enc_slot, enc_slot_node, mesh_nodes, mesh_edges,
     mesh_sender, mesh_receiver, mesh_send_node, grid_w, enc_w, node_w, proc_w, final_w,
     biases, gains,
-    grid_out, mesh_out,
+    v_go, v_mo,
     v_grid, v_ee, v_esnd, v_eslot, v_esn, v_mesh, v_me, v_msnd, v_mrcv, v_msn,
-    v_gw, v_ew, v_nw, v_pw, v_fw, v_bias, v_gain, v_go, v_mo,
+    v_gw, v_ew, v_nw, v_pw, v_fw, v_bias, v_gain,
     keys, arrived, ssum, landed, part, came, mid, srows, arr, arr2,
     part2, far2, near2, relay2, relayed2,
     g_key, g_slot, s_slot, g_snd, p_node, g_send, g_msnd, g_rcv, r_rcv,
     sproj, acc, acc2, opart, msg, base_mid, base_fin, gsel, tkeys,
-    load_sem, out_sem, ka_s, ka_r, cs_s, cs_r, rs_s, rs_r, ag_s, ag_r, aa_s, aa_r, rt_s, rt_r,
+    load_sem, ka_s, ka_r, cs_s, cs_r, rs_s, rs_r, ag_s, ag_r, aa_s, aa_r, rt_s, rt_r,
 ):
     n_blk = lax.axis_size("blk")
     n_band = lax.axis_size("band")
@@ -359,8 +359,6 @@
         tail = norm(dot(silu(first).astype(BF), v_gw[1]) + v_bias[0, 1:2, :], v_gain[0:1, :])
         v_go[rows, :] = (v_grid[rows, :].astype(F32) + tail).astype(BF)
 
-    grid_copy = pltpu.make_async_copy(v_go, grid_out, out_sem.at[0])
-    grid_copy.start()
     ready("fw")
     base_fin[...] = dot(mid[band], v_fw[0]) + v_bias[4, 0:1, :]
 
@@ -405,31 +403,20 @@
     tail = norm(dot(silu(first).astype(BF), v_fw[2]) + v_bias[4, 1:2, :], v_gain[4:5, :])
     for c in range(NC):
         v_mo[:, cols[c]] = (mid[band, :, cols[c]].astype(F32) + tail[:, cols[c]]).astype(BF)
-    mesh_copy = pltpu.make_async_copy(v_mo, mesh_out, out_sem.at[1])
-    mesh_copy.start()
     for copy in sent:
         copy.wait_send()
     for copy in everyone:
         copy.wait_send()
-    grid_copy.wait()
-    mesh_copy.wait()
-
-
-def handed_on(grid_in, mesh_in, grid_out, mesh_out, v_mesh, v_grid, sem):
-    pieces = v_grid.shape[0]
-    rows = v_grid.shape[1]
-    copies = [(mesh_in, v_mesh, mesh_out)]
-    for i in range(pieces):
-        part = pl.ds(i * rows, rows)
-        copies.append((grid_in.at[part], v_grid.at[i], grid_out.at[part]))
-    come = [pltpu.make_async_copy(a, v, sem.at[0, i]) for i, (a, v, _) in enumerate(copies)]
-    leave = [pltpu.make_async_copy(v, b, sem.at[1, i]) for i, (_, v, b) in enumerate(copies)]
-    for copy in come:
+
+
+def handed_on(v_grid, v_mesh, grid_out, mesh_out, sem):
+    copies = [
+        pltpu.make_async_copy(v_mesh, mesh_out, sem.at[0]),
+        pltpu.make_async_copy(v_grid, grid_out, sem.at[1]),
+    ]
+    for copy in copies:
         copy.start()
-    for first, second in zip(come, leave):
-        first.wait()
-        second.start()
-    for copy in leave:
+    for copy in copies:
         copy.wait()
 
 
@@ -453,7 +440,6 @@
     vm = pltpu.VMEM
     dma = pltpu.SemaphoreType.DMA
     scratch = [vm(a.shape, a.dtype) for a in args]
-    scratch += [vm((grid_rows, width), BF), vm((share, width), BF)]
     window = (NC, NEIGH, CAP, wc)
     shares, piece = (NC, n_band, share, wc), (NC, share, wc)
     boxes = (NC, n_blk, requests // n_blk, wc)
@@ -473,22 +459,20 @@
         vm((share, width), F32), vm((slots, width), BF), vm((nodes, width), BF),
     ]
     near = len(WINDOWS)
-    scratch += [dma((24,)), dma((2,))]
+    scratch += [dma((24,))]
     scratch += [dma((NC, near))] * 2 + [dma((NS, near))] * 2
     scratch += [dma((NS, 3))] * 2 + [dma((NM, 3))] * 2
     scratch += [dma((NC,))] * 2 + [dma((NC, 3))] * 2
     anywhere = pl.BlockSpec(memory_space=pl.ANY)
+    on_chip = pl.BlockSpec(memory_space=pltpu.VMEM)
     results = pl.pallas_call(
         kernel,
-        out_shape=(
-            jax.ShapeDtypeStruct((grid_rows, width), BF),
-            jax.ShapeDtypeStruct((share, width), BF),
-        ),
+        out_shape=(vm((grid_rows, width), BF), vm((share, width), BF)),
         in_specs=[anywhere] * len(args),
-        out_specs=(anywhere, anywhere),
+        out_specs=(on_chip, on_chip),
         scratch_shapes=scratch,
         compiler_params=pltpu.CompilerParams(
-            collective_id=0, has_side_effects=True, vmem_limit_bytes=56 * 1024 * 1024
+            collective_id=0, has_side_effects=True, vmem_limit_bytes=60 * 1024 * 1024
         ),
         name="encoder_processor",
     )(*args)
@@ -497,9 +481,9 @@
         out_shape=tuple(jax.ShapeDtypeStruct(r.shape, r.dtype) for r in results),
         in_specs=[anywhere] * 2,
         out_specs=(anywhere, anywhere),
-        scratch_shapes=[vm((share, width), BF), vm((4, grid_rows // 4, width), BF), dma((2, 5))],
+        scratch_shapes=[dma((2,))],
         name="handed_on",
-    )(*results)
+    )(*[pltpu.with_memory_space_constraint(r, pltpu.VMEM) for r in results])
 
 
 def solution(mesh):

time: 76.5 us -> 74.9 us (0.979)
  Pallas kernels: 75.6 us -> 74 us
    pallas_call x1, Pallas kernels: 1.92 us -> 0.87 us  [per_device(): pl.pallas_call(handed_on, out_shape=tuple((jax.ShapeDtypeStruct(r.shape,...]
where the time goes in v4:
time: 74.9 us; the launch traced here: 74.8 us
  Pallas kernels  74 us (99%)
  between operations  0.81 us (1%)
    pallas_call x1, Pallas kernels, per_device(): pl.pallas_call(kernel, out_shape=(vm((grid_rows, width), BF), vm((share,...  73.1 us

profile of v4, /device:TPU:32, one launch (start us, length us, event | category | flops | bytes accessed | tf_op | source)
XLA Modules:
  0.0 74.8 jit_solution(14610916888352371989)
XLA Ops:
  0.6 73.1 %encoder_processor.1 = (bf16[512,512]{1,0:T(8,128)(2,1)S(1)}, bf16[160,512]{1,0:T(8,128)(2,1)S(1)}) custom-call(bf16[512,512]{1,0:T(8,128)(2,1)} %grid_nodes.1, bf16[1024,512]{1,0:T(8,128)(2,1)} %enc_edges.1, s32[8,128]{1,0:T(8,128)} %bitcast.4, s32[8,128]{1,0:T(8,128)} %bitcast.5, s32[1,512]{1,0:T(1,128)} %enc_slot_node.1, bf16[640,512]{1,0:T(8,128)(2,1)} %mesh_nodes.1, ...), custom_call_target="tpu_custom_call" | custom-call | tf_op jit(solution)/shard_map/encoder_processor/pallas_call | solution.py:468
  73.8 0.9 %handed_on.1 = (bf16[512,512]{1,0:T(8,128)(2,1)}, bf16[160,512]{1,0:T(8,128)(2,1)}) custom-call(bf16[512,512]{1,0:T(8,128)(2,1)S(1)} %get-tuple-element.4.v_grid, bf16[160,512]{1,0:T(8,128)(2,1)S(1)} %get-tuple-element.5.v_mesh), custom_call_target="tpu_custom_call" | custom-call | tf_op jit(solution)/shard_map/handed_on/pallas_call | solution.py:479

commit v5 on v4

--- a/solution.py
+++ b/solution.py
@@ -8,7 +8,7 @@
 NEIGH = 8
 CAP = 64
 MIDDLE = NEIGH // 2
-WINDOWS = [k for k in range(NEIGH) if k != MIDDLE]
+WINDOWS = [0, 1, 7, 2, 6, 5, 3]
 NC = 2
 NS = 4
 NM = 4
@@ -242,7 +242,8 @@
             acc2[rows, :] = dot(v_me[rows, :], v_pw[0]) + v_bias[3, 0:1, :]
             g_msnd[rows, :] = rows_select(down_column(v_msnd[pl.ds(r, 1), :]), slots)
 
-    fills = [fill_base, fill_send, lambda: fill_edges(0, 2), lambda: fill_edges(1, 2)]
+    fill_base()
+    fill_send()
 
     def toward(c):
         return (left, right) if c == 0 else (right, left)
@@ -252,7 +253,6 @@
         far_copy = remote(part.at[c, across], far.at[c], sem_s.at[c, 0], sem_r.at[c, 0], blk, first)
         near_copy = remote(part.at[c, other], near.at[c], sem_s.at[c, 1], sem_r.at[c, 1], blk, other)
         far_copy.start()
-        near_copy.start()
         return far_copy, near_copy
 
     def scatter_relay(c, far_copy, part, far, relay, relayed, sem_s, sem_r):
@@ -276,8 +276,6 @@
             copies.append(copy)
         pieces.append(copies)
         sent += copies
-        if c < NS - 1:
-            fills[c]()
 
     first = base_mid[...]
     for c in range(NS):
@@ -337,7 +335,7 @@
     to_everyone(0)
     pick(1, halves[1])
     to_everyone(1)
-    fills[NS - 1]()
+    fill_edges(0, 1)
     sent += list(gathers.values())
 
     tkeys[...] = dot(mid[...].reshape(nodes, width), v_pw[2]).astype(BF)
@@ -390,10 +388,13 @@
         sums = dot(r_rcv[...], msg[:, cols[c]]).astype(BF)
         part2[c] = sums.reshape(n_band, share, wc)
         scatters.append(scatter_start(c, part2, far2, near2, rt_s, rt_r))
+    for far_copy, near_copy in scatters:
+        far_copy.wait_send()
+        near_copy.start()
     relays = []
     for c in range(NC):
         relays.append(scatter_relay(c, scatters[c][0], part2, far2, relay2, relayed2, rt_s, rt_r))
-        sent += [*scatters[c], relays[c]]
+        sent += [scatters[c][1], relays[c]]
     first = base_fin[...]
     for c in range(NC):
         scatters[c][1].wait_recv()

time: 74.9 us -> 74.6 us (level)
  no operation moved by 1% of the time
where the time goes in v5:
time: 74.6 us; the launch traced here: 74.5 us
  Pallas kernels  73.7 us (99%)
  between operations  0.81 us (1%)
    pallas_call x1, Pallas kernels, per_device(): pl.pallas_call(kernel, out_shape=(vm((grid_rows, width), BF), vm((share,...  72.8 us

profile of v5, /device:TPU:32, one launch (start us, length us, event | category | flops | bytes accessed | tf_op | source)
XLA Modules:
  0.0 74.5 jit_solution(7872050737398118522)
XLA Ops:
  0.6 72.8 %encoder_processor.1 = (bf16[512,512]{1,0:T(8,128)(2,1)S(1)}, bf16[160,512]{1,0:T(8,128)(2,1)S(1)}) custom-call(bf16[512,512]{1,0:T(8,128)(2,1)} %grid_nodes.1, bf16[1024,512]{1,0:T(8,128)(2,1)} %enc_edges.1, s32[8,128]{1,0:T(8,128)} %bitcast.4, s32[8,128]{1,0:T(8,128)} %bitcast.5, s32[1,512]{1,0:T(1,128)} %enc_slot_node.1, bf16[640,512]{1,0:T(8,128)(2,1)} %mesh_nodes.1, ...), custom_call_target="tpu_custom_call" | custom-call | tf_op jit(solution)/shard_map/encoder_processor/pallas_call | solution.py:469
  73.4 0.9 %handed_on.1 = (bf16[512,512]{1,0:T(8,128)(2,1)}, bf16[160,512]{1,0:T(8,128)(2,1)}) custom-call(bf16[512,512]{1,0:T(8,128)(2,1)S(1)} %get-tuple-element.4.v_grid, bf16[160,512]{1,0:T(8,128)(2,1)S(1)} %get-tuple-element.5.v_mesh), custom_call_target="tpu_custom_call" | custom-call | tf_op jit(solution)/shard_map/handed_on/pallas_call | solution.py:480

commit v6 on v5

--- a/solution.py
+++ b/solution.py
@@ -248,13 +248,6 @@
     def toward(c):
         return (left, right) if c == 0 else (right, left)
 
-    def scatter_start(c, part, far, near, sem_s, sem_r):
-        first, other = toward(c)
-        far_copy = remote(part.at[c, across], far.at[c], sem_s.at[c, 0], sem_r.at[c, 0], blk, first)
-        near_copy = remote(part.at[c, other], near.at[c], sem_s.at[c, 1], sem_r.at[c, 1], blk, other)
-        far_copy.start()
-        return far_copy, near_copy
-
     def scatter_relay(c, far_copy, part, far, relay, relayed, sem_s, sem_r):
         first, _ = toward(c)
         far_copy.wait_recv()
@@ -270,7 +263,7 @@
         sums = dot(p_node[...], landed[c].reshape(slots, ws)).astype(BF)
         part[c] = sums.reshape(n_band, share, ws)
         copies = []
-        for i, peer in enumerate((right, left, across)):
+        for i, peer in enumerate((across, right, left)):
             copy = remote(part.at[c, peer], came.at[c, i], rs_s.at[c, i], rs_r.at[c, i], blk, peer)
             copy.start()
             copies.append(copy)
@@ -385,9 +378,19 @@
 
     scatters = []
     for c in range(NC):
-        sums = dot(r_rcv[...], msg[:, cols[c]]).astype(BF)
-        part2[c] = sums.reshape(n_band, share, wc)
-        scatters.append(scatter_start(c, part2, far2, near2, rt_s, rt_r))
+        def shared(peer):
+            rows = pl.ds(pl.multiple_of(peer * share, 32), share)
+            part2[c, peer] = dot(r_rcv[rows, :], msg[:, cols[c]]).astype(BF)
+
+        shared(across)
+        towards, other = toward(c)
+        far_copy = remote(part2.at[c, across], far2.at[c], rt_s.at[c, 0], rt_r.at[c, 0], blk, towards)
+        near_copy = remote(part2.at[c, other], near2.at[c], rt_s.at[c, 1], rt_r.at[c, 1], blk, other)
+        far_copy.start()
+        shared(other)
+        shared(towards)
+        shared(band)
+        scatters.append((far_copy, near_copy))
     for far_copy, near_copy in scatters:
         far_copy.wait_send()
         near_copy.start()

time: 74.6 us -> 73.7 us (0.988)
  Pallas kernels: 73.7 us -> 72.8 us
    pallas_call x1, Pallas kernels: 72.8 us -> 71.9 us  [per_device(): pl.pallas_call(kernel, out_shape=(vm((grid_rows, width), BF), vm((share,...]
where the time goes in v6:
time: 73.7 us; the launch traced here: 73.6 us
  Pallas kernels  72.8 us (99%)
  between operations  0.81 us (1%)
    pallas_call x1, Pallas kernels, per_device(): pl.pallas_call(kernel, out_shape=(vm((grid_rows, width), BF), vm((share,...  71.9 us

profile of v6, /device:TPU:32, one launch (start us, length us, event | category | flops | bytes accessed | tf_op | source)
XLA Modules:
  0.0 73.6 jit_solution(15439166417101747757)
XLA Ops:
  0.6 71.9 %encoder_processor.1 = (bf16[512,512]{1,0:T(8,128)(2,1)S(1)}, bf16[160,512]{1,0:T(8,128)(2,1)S(1)}) custom-call(bf16[512,512]{1,0:T(8,128)(2,1)} %grid_nodes.1, bf16[1024,512]{1,0:T(8,128)(2,1)} %enc_edges.1, s32[8,128]{1,0:T(8,128)} %bitcast.4, s32[8,128]{1,0:T(8,128)} %bitcast.5, s32[1,512]{1,0:T(1,128)} %enc_slot_node.1, bf16[640,512]{1,0:T(8,128)(2,1)} %mesh_nodes.1, ...), custom_call_target="tpu_custom_call" | custom-call | tf_op jit(solution)/shard_map/encoder_processor/pallas_call | solution.py:472
  72.6 0.9 %handed_on.1 = (bf16[512,512]{1,0:T(8,128)(2,1)}, bf16[160,512]{1,0:T(8,128)(2,1)}) custom-call(bf16[512,512]{1,0:T(8,128)(2,1)S(1)} %get-tuple-element.4.v_grid, bf16[160,512]{1,0:T(8,128)(2,1)S(1)} %get-tuple-element.5.v_mesh), custom_call_target="tpu_custom_call" | custom-call | tf_op jit(solution)/shard_map/handed_on/pallas_call | solution.py:483
